TPU v7x, 512 devices: a whole 4x4x16 slice. The times are simulated.
512 devices in a mesh: segment: 8 (over z_lo), seq: 16 (over z_hi, y, core), head: 4 (over x).
Axes of the slice: x: 4, y: 4, z: 16 (z_hi: 2, z_lo: 8; z = z_hi * 8 + z_lo), core: 2. Of those that a mesh axis runs over, the one named last changes fastest.
Arguments:
- tokens: bfloat16 [8, 4096, 1536], P('segment', ('seq', 'head'))
- lengths: int32 [8], replicated, may hold values from 2048 to 4096, as said below
- modulation: bfloat16 [8, 2, 1536], P('segment'), may hold values from -0.5 to 0.5
- gate_gain: bfloat16 [8, 1536], P('segment'), may hold values from 1 to 3
- w_qkv: bfloat16 [8, 1536, 3, 1536], P('segment', None, None, 'head')
- w_out: bfloat16 [8, 1536, 1536], P('segment', 'head'), may hold values from -0.15625 to 0.15625
Outputs:
- states: bfloat16 [8, 4096, 1536], P('segment', ('seq', 'head'))
Inputs may be any that keep to these rules, and one draw needn't show every extreme that they name: Micro-batch m has lengths[m] real tokens at the start of its 4096 slots; some micro-batch fills all 4096.
All inputs are finite; a program needn't handle non-finite values.
Results may differ from a plain program's by a relative error of at most 0.02.
Values may be sent and summed in bfloat16 or wider, within the bound.
A program may use at most 64 MiB of HBM per device.

v0:
```python
import jax
import jax.numpy as jnp
from jax import lax
from jax.sharding import PartitionSpec as P

HEAD = 128
TICKS = 2


def from_behind(value, axis, by):
    length = lax.axis_size(axis)
    return lax.ppermute(value, axis, [(i, (i + by) % length) for i in range(length)])


def layer_norm(values):
    row_mean = jnp.mean(values, axis=-1, keepdims=True)
    centered = values - row_mean
    row_var = jnp.mean(centered * centered, axis=-1, keepdims=True)
    return centered / jnp.sqrt(row_var + 1e-06)


def block_size(key_count, shard_rows):
    for candidate in (1024, 512):
        return candidate
    if key_count <= 1024:
        return key_count
    return shard_rows


def attend_block(running, query_heads, key_block, value_block, first_row, length, score_scale):
    row_max, row_sum, weighted = running
    key_count = key_block.shape[0]
    local_heads = query_heads.shape[1]
    head_size = query_heads.shape[2]
    key_heads = key_block.reshape(key_count, local_heads, head_size)
    value_heads = value_block.reshape(key_count, local_heads, head_size)
    scores = (
        jnp.einsum("rhd,khd->hrk", query_heads, key_heads, preferred_element_type=jnp.float32)
        * score_scale
    )
    key_valid = first_row + jnp.arange(key_count, dtype=jnp.int32) < length
    scores = jnp.where(key_valid[None, None, :], scores, -1e30)
    new_max = jnp.maximum(row_max, jnp.max(scores, axis=2))
    exponent = jnp.where(key_valid[None, None, :], jnp.exp(scores - new_max[:, :, None]), 0.0)
    rescale = jnp.exp(row_max - new_max)
    row_sum = row_sum * rescale + jnp.sum(exponent, axis=2)
    weighted = weighted * rescale[:, :, None] + jnp.einsum(
        "hrk,khd->hrd",
        exponent.astype(jnp.bfloat16),
        value_heads,
        preferred_element_type=jnp.float32,
    )
    return (new_max, row_sum, weighted)


def attend_piece(running, pieces, query_heads, length, score_scale, shard_rows):
    key_piece, value_piece = pieces
    key_count = key_piece.shape[0]
    block = block_size(key_count, shard_rows)
    blocks = key_count // block
    key_stack = key_piece.reshape(blocks, block, key_piece.shape[1])
    value_stack = value_piece.reshape(blocks, block, value_piece.shape[1])

    def step_block(state_now, inputs):
        key_block, value_block, block_index = inputs
        return (
            attend_block(
                state_now,
                query_heads,
                key_block,
                value_block,
                block_index * block,
                length,
                score_scale,
            ),
            None,
        )

    final, unused = lax.scan(
        step_block, running, (key_stack, value_stack, jnp.arange(blocks, dtype=jnp.int32))
    )
    return final


def per_device(tokens, lengths, modulation, gate_gain, w_qkv, w_out):
    segment_count = lax.axis_size("segment")
    position = lax.axis_index("segment")
    state = tokens[0]
    shift_scale = modulation[0].astype(jnp.float32)
    gate_row = gate_gain[0].astype(jnp.float32)
    model_width = w_qkv.shape[1]
    local_width = w_qkv.shape[3]
    local_heads = local_width // HEAD
    flat_qkv = w_qkv[0].reshape(model_width, 3 * local_width)
    out_heads = w_out[0].reshape(local_heads, HEAD, model_width)
    score_scale = HEAD ** (-0.5)
    for tick_index in range(TICKS):
        micro_index = (position - tick_index) % segment_count
        length = lax.dynamic_index_in_dim(lengths, micro_index, 0, keepdims=False)
        values = state.astype(jnp.float32)
        normed = (layer_norm(values) * (1.0 + shift_scale[1]) + shift_scale[0]).astype(jnp.bfloat16)
        projected = jnp.dot(
            lax.all_gather(normed, "head", axis=0, tiled=True),
            flat_qkv,
            preferred_element_type=jnp.float32,
        ).astype(jnp.bfloat16)
        query_rows = projected.shape[0]
        query_heads = projected[:, :local_width].reshape(query_rows, local_heads, HEAD)
        key_part = projected[:, local_width : 2 * local_width]
        value_part = projected[:, 2 * local_width :]
        initial = (
            jnp.full((local_heads, query_rows), -1e30, jnp.float32),
            jnp.zeros((local_heads, query_rows), jnp.float32),
            jnp.zeros((local_heads, query_rows, HEAD), jnp.float32),
        )
        running = attend_piece(
            initial,
            (
                lax.all_gather(key_part, "seq", axis=0, tiled=True),
                lax.all_gather(value_part, "seq", axis=0, tiled=True),
            ),
            query_heads,
            length,
            score_scale,
            query_rows,
        )
        attended = (running[2] / running[1][:, :, None]).astype(jnp.bfloat16)
        branch = lax.psum_scatter(
            jnp.einsum(
                "hrd,hdn->rn", attended, out_heads, preferred_element_type=jnp.float32
            ).astype(jnp.bfloat16),
            "head",
            scatter_dimension=0,
            tiled=True,
        ).astype(jnp.float32)
        updated = (values + gate_row * branch).astype(jnp.bfloat16)
        state = from_behind(updated, "segment", 1)
    return state[None]


def solution(mesh):
    return jax.shard_map(
        per_device,
        mesh=mesh,
        in_specs=(
            P("segment", ("seq", "head"), None),
            P(),
            P("segment", None, None),
            P("segment", None),
            P("segment", None, None, "head"),
            P("segment", "head", None),
        ),
        out_specs=P("segment", ("seq", "head"), None),
        check_vma=False,
    )
```

profile of v0, /device:TPU:8, one launch (start us, length us, event | category | flops | bytes accessed | tf_op | source)
XLA Modules:
  0.0 673.3 jit_solution(7717919724192401937)
XLA Ops:
  10.7 13.7 %all_gather.18 = bf16[256,1536]{1,0:T(8,128)(2,1)S(1)} all-gather(bf16[64,1536]{1,0:T(8,128)(2,1)S(1)} %fusion.45), channel_id=1, replica_groups=mesh['segment'=8,'seq'=16,'head'=4] {'head'}, dimensions={0}, use_global_device_ids=true | all-gather | bytes 983040 | tf_op jit(solution)/shard_map/all_gather | solution.py:103
  24.4 6.1 copy.17
  37.0 108.7 %all-gather.5.cloned.1.call-done = bf16[4096,384]{1,0:T(8,128)(2,1)} async-done(((bf16[256,384]{1,0:T(8,128)(2,1)}), bf16[4096,384]{1,0:T(8,128)(2,1)}) %all-gather.5.cloned.1.call-update) | async-done | bytes 3145744 | tf_op jit(solution)/shard_map/all_gather | solution.py:119
  145.6 101.3 %all-gather.7.cloned.1.call-done = bf16[4096,384]{1,0:T(8,128)(2,1)} async-done(((bf16[256,384]{1,0:T(8,128)(2,1)}), bf16[4096,384]{1,0:T(8,128)(2,1)}) %all-gather.7.cloned.1.call-update) | async-done | bytes 3145744 | tf_op jit(solution)/shard_map/all_gather | solution.py:120
  246.9 56.6 %while.30 = (s32[]{:T(128)}, f32[3,256]{1,0:T(4,128)S(1)}, f32[3,256]{1,0:T(4,128)S(1)}, f32[3,256,128]{2,1,0:T(8,128)}, s32[4]{0:T(128)S(1)}, /*index=5*/s32[]{...) while((s32[]{:T(128)}, f32[3,256]{1,0:T(4,128)S(1)}, ...), condition=%wide.region_5.6_spmd.clone, body=%wide.region_2.5_spmd.clone.sunk | while | flops 413177600 | bytes 21483740 | solution.py:79
  250.6 3.4 bitcast_reduce_fusion.4
  256.9 3.4 fusion.86
  264.7 3.4 bitcast_reduce_fusion.4
  271.0 3.4 fusion.86
  278.9 3.4 bitcast_reduce_fusion.4
  285.2 3.4 fusion.86
  293.0 3.4 bitcast_reduce_fusion.4
  299.3 3.4 fusion.86
  306.2 21.7 %reduce-scatter.3.cloned.1.call-done = bf16[64,1536]{1,0:T(8,128)(2,1)} async-done(((bf16[256,1536]{1,0:T(8,128)(2,1)}), bf16[64,1536]{1,0:T(8,128)(2,1)}) %reduce-scatter.3.cloned.1.call-update) | async-done | bytes 196624 | tf_op jit(solution)/shard_map/reduce_scatter | solution.py:128
  329.0 3.5 collective-permute-start
  332.4 11.0 %collective-permute-done = bf16[64,1536]{1,0:T(8,128)(2,1)S(1)} collective-permute-done((bf16[64,1536]{1,0:T(8,128)(2,1)S(1)}, bf16[64,1536]{1,0:T(8,128)(2,1)S(1)}, u32[]{:S(2)}, u32[]{:S(2)}) %collective-permute-start) | collective-permute-done | bytes 196640 | tf_op jit(solution)/shard_map/ppermute | solution.py:12
  344.2 13.6 %all_gather.21 = bf16[256,1536]{1,0:T(8,128)(2,1)S(1)} all-gather(bf16[64,1536]{1,0:T(8,128)(2,1)S(1)} %fusion.41), channel_id=1, replica_groups=mesh['segment'=8,'seq'=16,'head'=4] {'head'}, dimensions={0}, use_global_device_ids=true | all-gather | bytes 983040 | tf_op jit(solution)/shard_map/all_gather | solution.py:103
  357.9 3.2 convolution_convert_fusion
  363.6 104.3 %all-gather.11.cloned.1.call-done = bf16[4096,384]{1,0:T(8,128)(2,1)} async-done(((bf16[256,384]{1,0:T(8,128)(2,1)}), bf16[4096,384]{1,0:T(8,128)(2,1)}) %all-gather.11.cloned.1.call-update) | async-done | bytes 3145744 | tf_op jit(solution)/shard_map/all_gather | solution.py:120
  467.9 101.2 %all-gather.9.cloned.1.call-done = bf16[4096,384]{1,0:T(8,128)(2,1)} async-done(((bf16[256,384]{1,0:T(8,128)(2,1)}), bf16[4096,384]{1,0:T(8,128)(2,1)}) %all-gather.9.cloned.1.call-update) | async-done | bytes 3145744 | tf_op jit(solution)/shard_map/all_gather | solution.py:119
  569.1 56.8 %while.31 = (s32[]{:T(128)}, f32[3,256]{1,0:T(4,128)S(1)}, f32[3,256]{1,0:T(4,128)S(1)}, f32[3,256,128]{2,1,0:T(8,128)}, s32[4]{0:T(128)S(1)}, /*index=5*/s32[]{...) while((s32[]{:T(128)}, f32[3,256]{1,0:T(4,128)S(1)}, ...), condition=%wide.region_12.13_spmd.clone, body=%wide.region_9.12_spmd.clone.sunk | while | flops 413177600 | bytes 21483740 | solution.py:79
  572.8 3.5 bitcast_reduce_fusion.5
  579.1 3.4 fusion.93
  587.0 3.5 bitcast_reduce_fusion.5
  593.3 3.4 fusion.93
  601.2 3.5 bitcast_reduce_fusion.5
  607.5 3.4 fusion.93
  615.4 3.5 bitcast_reduce_fusion.5
  621.7 3.4 fusion.93
  628.5 21.8 %reduce-scatter.5.cloned.1.call-done = bf16[64,1536]{1,0:T(8,128)(2,1)} async-done(((bf16[256,1536]{1,0:T(8,128)(2,1)}), bf16[64,1536]{1,0:T(8,128)(2,1)}) %reduce-scatter.5.cloned.1.call-update) | async-done | bytes 196624 | tf_op jit(solution)/shard_map/reduce_scatter | solution.py:128
  651.3 3.5 collective-permute-start.1
  654.8 11.0 %collective-permute-done.1 = bf16[64,1536]{1,0:T(8,128)(2,1)S(1)} collective-permute-done((bf16[64,1536]{1,0:T(8,128)(2,1)S(1)}, bf16[64,1536]{1,0:T(8,128)(2,1)S(1)}, u32[]{:S(2)}, u32[]{:S(2)}) %collective-permute-start.1) | collective-permute-done | bytes 196640 | tf_op jit(solution)/shard_map/ppermute | solution.py:12
  (174 shorter events, 74.4 us)
Async XLA Ops:
  6.5 297.0 %copy-start = (bf16[1,384,1536]{2,1,0:T(8,128)(2,1)S(1)}, bf16[1,384,1536]{2,1,0:T(8,128)(2,1)}, u32[]{:S(2)}) copy-start(bf16[1,384,1536]{2,1,0:T(8,128)(2,1)} %param.15) | copy-start | bytes 3538948
  6.5 139.1 %all-gather.5.cloned.1.call-start = ((), (), s32[]{:S(2)}) async-start(), calls=%async_computation.2 | async-start | bytes 3342336 | tf_op jit(solution)/shard_map/all_gather | solution.py:119
  7.4 2.3 copy-start.6
  7.4 3.3 copy-start.8
  30.5 5.9 copy-start.11
  34.5 212.4 %all-gather.7.cloned.1.call-start = ((), (), s32[]{:S(2)}) async-start(), calls=%async_computation.3 | async-start | bytes 3342336 | tf_op jit(solution)/shard_map/all_gather | solution.py:120
  35.3 292.7 %reduce-scatter.3.cloned.1.call-start = ((), (), s32[]{:S(2)}) async-start(), calls=%async_computation.4 | async-start | bytes 983040 | tf_op jit(solution)/shard_map/reduce_scatter | solution.py:128
  254.0 2.8 copy-start.12
  260.3 0.8 copy-start.13
  268.2 2.8 copy-start.12
  274.4 0.8 copy-start.13
  282.3 2.8 copy-start.12
  288.6 0.8 copy-start.13
  296.5 2.8 copy-start.12
  302.7 0.8 copy-start.13
  303.5 2.7 copy-start.10
  303.5 24.4 %copy-start.1 = (bf16[1,64,1536]{2,1,0:T(8,128)(2,1)S(1)}, bf16[1,64,1536]{2,1,0:T(8,128)(2,1)}, u32[]{:S(2)}) copy-start(bf16[1,64,1536]{2,1,0:T(8,128)(2,1)} %param.10) | copy-start | bytes 589828
  303.5 40.5 %copy-start.7 = (f32[1536]{0:T(1024)S(1)}, f32[1536]{0:T(1024)}, u32[]{:S(2)}) copy-start(f32[1536]{0:T(1024)} %copy-done.6) | copy-start | bytes 18436
  303.5 40.5 %copy-start.9 = (f32[1536]{0:T(1024)S(1)}, f32[1536]{0:T(1024)}, u32[]{:S(2)}) copy-start(f32[1536]{0:T(1024)} %copy-done.8) | copy-start | bytes 18436
  306.1 161.8 %all-gather.11.cloned.1.call-start = ((), (), s32[]{:S(2)}) async-start(), calls=%async_computation.6 | async-start | bytes 3342336 | tf_op jit(solution)/shard_map/all_gather | solution.py:120
  306.2 54.9 %copy-start.4 = (f32[1536]{0:T(1024)}, f32[1536]{0:T(1024)S(1)}, u32[]{:S(2)}) copy-start(f32[1536]{0:T(1024)S(1)} %convert_reduce_fusion.2) | copy-start | bytes 18436
  329.0 14.4 %collective-permute-start = (bf16[64,1536]{1,0:T(8,128)(2,1)S(1)}, bf16[64,1536]{1,0:T(8,128)(2,1)S(1)}, u32[]{:S(2)}, u32[]{:S(2)}) collective-permute-start(bf16[64,1536]{1,0:T(8,128)(2,1)S(1)} %fusion.46), channel_id=1, source_target_pairs={{0,64},{64,128},{128,192},{192,256},{256,320},{320,384},{384,448},... | collective-permute-start | bytes 589832 | tf_op jit(solution)/shard_map/ppermute | solution.py:12
  362.0 207.1 %all-gather.9.cloned.1.call-start = ((), (), s32[]{:S(2)}) async-start(), calls=%async_computation.5 | async-start | bytes 3342336 | tf_op jit(solution)/shard_map/all_gather | solution.py:119
  362.6 287.7 %reduce-scatter.5.cloned.1.call-start = ((), (), s32[]{:S(2)}) async-start(), calls=%async_computation.7 | async-start | bytes 983040 | tf_op jit(solution)/shard_map/reduce_scatter | solution.py:128
  576.3 2.8 copy-start.14
  582.6 0.7 copy-start.15
  590.5 2.8 copy-start.14
  604.7 2.8 copy-start.14
  618.9 2.8 copy-start.14
  625.9 24.4 %copy-start.3 = (bf16[64,1536]{1,0:T(8,128)(2,1)S(1)}, bf16[64,1536]{1,0:T(8,128)(2,1)}, u32[]{:S(2)}) copy-start(bf16[64,1536]{1,0:T(8,128)(2,1)} %copy-done.2) | copy-start | bytes 589828
  625.9 24.4 %copy-start.5 = (f32[1536]{0:T(1024)S(1)}, f32[1536]{0:T(1024)}, u32[]{:S(2)}) copy-start(f32[1536]{0:T(1024)} %copy-done.4) | copy-start | bytes 18436
  651.3 14.5 %collective-permute-start.1 = (bf16[64,1536]{1,0:T(8,128)(2,1)S(1)}, bf16[64,1536]{1,0:T(8,128)(2,1)S(1)}, u32[]{:S(2)}, u32[]{:S(2)}) collective-permute-start(bf16[64,1536]{1,0:T(8,128)(2,1)S(1)} %fusion.47), channel_id=1, source_target_pairs={{0,64},{64,128},{128,192},{192,256},{256,320},{320,384},{384,448},... | collective-permute-start | bytes 589832 | tf_op jit(solution)/shard_map/ppermute | solution.py:12
  (4 other events, 2.9 us)
Sparse Core Ops, SparseCore 0:
  34.7 110.9 all-gather.4
  148.9 97.9 all-gather.6
  306.3 21.6 reduce-scatter.2
  362.1 105.7 all-gather.10
  471.1 97.9 all-gather.8
  628.6 21.6 reduce-scatter.4
where the time goes:
time: 674 us; the launch traced here: 673 us
  waiting for transfers between devices  482 us (72%)
  matrix products  66.5 us (10%)
  local copies, waits for them, and re-layouts  39 us (6%)
  other arithmetic  31.6 us (5%)
  blocking collectives  27.3 us (4%)
  between operations  13.7 us (2%)
  starting transfers between devices  7.13 us (1%)
    all_gather x2, waiting for transfers between devices, per_device(): lax.all_gather(key_part, 'seq', axis=0, tiled=True)  210 us
    all_gather x2, waiting for transfers between devices, per_device(): lax.all_gather(value_part, 'seq', axis=0, tiled=True)  206 us
    reduce_scatter x2, waiting for transfers between devices, per_device(): lax.psum_scatter(jnp.einsum('hrd,hdn->rn', attended, out_heads, preferred...  43.5 us
    dot_general x8, matrix products, attend_block(): jnp.einsum('rhd,khd->hrk', query_heads, key_heads, preferred_element_type...  27.6 us
    dot_general x8, matrix products, attend_block(): jnp.einsum('hrk,khd->hrd', exponent.astype(jnp.bfloat16), value_heads, pr...  27.4 us
    all_gather x2, blocking collectives, per_device(): lax.all_gather(normed, 'head', axis=0, tiled=True)  27.3 us
    ppermute x2, waiting for transfers between devices, from_behind(): lax.ppermute(value, axis, [(i, (i + by) % length) for i in range(length)])  22 us
    dynamic_slice x32, local copies, waits for them, and re-layouts, attend_piece(): lax.scan(step_block, running, (key_stack, value_stack, jnp.arange(blocks,...  21.7 us
  transfers between devices with their start and end apart: 8, of which 8 were waited for; matrix products, arithmetic and copies ran while one was open for 0% of the time, Pallas kernels for 0%

commit v1 on v0

v1 whole, which is shorter than its diff:
```python
import functools
import math

import jax
import jax.numpy as jnp
from jax import lax
from jax.experimental import pallas as pl
from jax.experimental.pallas import tpu as pltpu
from jax.sharding import PartitionSpec as P

HEAD = 128
TICKS = 2
PLANE = 8
KEY_BLOCK = 1024
EXP2_SCALE = HEAD ** (-0.5) * math.log2(math.e)


def layer_norm(values):
    row_mean = jnp.mean(values, axis=-1, keepdims=True)
    centered = values - row_mean
    row_var = jnp.mean(centered * centered, axis=-1, keepdims=True)
    return centered / jnp.sqrt(row_var + 1e-06)


def attend_kernel(info_ref, q_ref, k_ref, v_ref, o_ref, max_ref, sum_ref, acc_ref):
    step = pl.program_id(1)
    length = info_ref[0]
    half = info_ref[1]

    @pl.when(step == 0)
    def _():
        max_ref[...] = jnp.full_like(max_ref, -1e30)
        sum_ref[...] = jnp.zeros_like(sum_ref)
        acc_ref[...] = jnp.zeros_like(acc_ref)

    row = lax.broadcasted_iota(jnp.int32, (1, KEY_BLOCK), 1) + step * KEY_BLOCK
    slot = jnp.bitwise_and(jnp.right_shift(row, 6), 1)
    which = jnp.bitwise_xor(slot, half)
    source = jnp.right_shift(row, 7)
    position = which * 2048 + source * 64 + jnp.bitwise_and(row, 63)
    valid = position < length

    scores = lax.dot_general(
        q_ref[...], k_ref[...], (((1,), (1,)), ((), ())), preferred_element_type=jnp.float32
    )
    scores = jnp.where(valid, scores * EXP2_SCALE, -1e30)
    old_max = max_ref[...]
    new_max = jnp.maximum(old_max, jnp.max(scores, axis=1, keepdims=True))
    rescale = jnp.exp2(old_max - new_max)
    weights = jnp.exp2(scores - new_max[:, :1])
    max_ref[...] = new_max
    sum_ref[...] = sum_ref[...] * rescale + jnp.sum(weights, axis=1, keepdims=True)
    acc_ref[...] = acc_ref[...] * rescale + jnp.dot(
        weights.astype(jnp.bfloat16), v_ref[...], preferred_element_type=jnp.float32
    )

    @pl.when(step == pl.num_programs(1) - 1)
    def _():
        o_ref[...] = (acc_ref[...] / sum_ref[...]).astype(o_ref.dtype)


def attend(info, queries, key_value):
    rows, width = queries.shape
    keys = key_value.shape[0]
    heads = width // HEAD
    return pl.pallas_call(
        attend_kernel,
        grid=(heads, keys // KEY_BLOCK),
        in_specs=[
            pl.BlockSpec(memory_space=pltpu.SMEM),
            pl.BlockSpec((rows, HEAD), lambda h, b: (0, h)),
            pl.BlockSpec((KEY_BLOCK, HEAD), lambda h, b: (b, h)),
            pl.BlockSpec((KEY_BLOCK, HEAD), lambda h, b: (b, heads + h)),
        ],
        out_specs=pl.BlockSpec((rows, HEAD), lambda h, b: (0, h)),
        out_shape=jax.ShapeDtypeStruct((rows, width), jnp.bfloat16),
        scratch_shapes=[pltpu.VMEM((rows, HEAD), jnp.float32)] * 3,
    )(info, queries, key_value, key_value)


def per_device(tokens, lengths, modulation, gate_gain, w_qkv, w_out):
    segment_count = lax.axis_size("segment")
    seq_count = lax.axis_size("seq")
    position = lax.axis_index("segment")
    half = lax.axis_index("seq") // PLANE
    groups = [list(range(PLANE)), list(range(PLANE, 2 * PLANE))]
    shift_scale = modulation[0].astype(jnp.float32)
    gate_row = gate_gain[0].astype(jnp.float32)
    model_width = w_qkv.shape[1]
    local_width = w_qkv.shape[3]
    flat_qkv = w_qkv[0].reshape(model_width, 3 * local_width)
    out_rows = w_out[0]
    own = tokens[0]
    other = lax.ppermute(own, "seq", [(i, (i + PLANE) % seq_count) for i in range(seq_count)])
    for tick_index in range(TICKS):
        micro_index = (position - tick_index) % segment_count
        length = lax.dynamic_index_in_dim(lengths, micro_index, 0, keepdims=False)
        info = jnp.stack([length, half.astype(jnp.int32)])
        values = own.astype(jnp.float32)
        both = jnp.concatenate([own, other], axis=0).astype(jnp.float32)
        normed = (layer_norm(both) * (1.0 + shift_scale[1]) + shift_scale[0]).astype(jnp.bfloat16)
        rows = lax.all_gather(normed, "head", axis=0, tiled=True)
        projected = jnp.dot(rows, flat_qkv, preferred_element_type=jnp.float32).astype(jnp.bfloat16)
        tile = own.shape[0]
        queries = projected[:, :local_width].reshape(-1, 2, tile, local_width)[:, 0]
        queries = queries.reshape(-1, local_width)
        key_value = lax.all_gather(
            projected[:, local_width:], "seq", axis=0, tiled=True, axis_index_groups=groups
        )
        attended = attend(info, queries, key_value)
        branch = lax.psum_scatter(
            jnp.dot(attended, out_rows, preferred_element_type=jnp.float32).astype(jnp.bfloat16),
            "head",
            scatter_dimension=0,
            tiled=True,
        ).astype(jnp.float32)
        updated = (values + gate_row * branch).astype(jnp.bfloat16)
        own = lax.ppermute(
            updated, "segment", [(i, (i + 1) % segment_count) for i in range(segment_count)]
        )
        if tick_index + 1 < TICKS:
            other = lax.ppermute(
                updated,
                ("segment", "seq"),
                [
                    (s * seq_count + q, (s + 1) % segment_count * seq_count + (q + PLANE) % seq_count)
                    for s in range(segment_count)
                    for q in range(seq_count)
                ],
            )
    return own[None]


def solution(mesh):
    return jax.shard_map(
        per_device,
        mesh=mesh,
        in_specs=(
            P("segment", ("seq", "head"), None),
            P(),
            P("segment", None, None),
            P("segment", None),
            P("segment", None, None, "head"),
            P("segment", "head", None),
        ),
        out_specs=P("segment", ("seq", "head"), None),
        check_vma=False,
    )
```

time: 674 us -> 378 us (0.56)
  waiting for transfers between devices: 482 us -> 267 us
  matrix products: 66.5 us -> 14.2 us
  local copies, waits for them, and re-layouts: 39 us -> 10.8 us
  blocking collectives: 27.3 us -> 0 us
  starting transfers between devices: 7.13 us -> 34.1 us
  Pallas kernels: 0 us -> 25.9 us
  other arithmetic: 31.6 us -> 10.6 us
    all_gather x4, waiting for transfers between devices: 415 us -> 160 us  [the longest x2 91.4 us: per_device(): lax.all_gather(projected[:, local_width:], 'seq', axis=0, tiled=True, axi...]
    dot_general x20 -> x4, matrix products: 66.5 us -> 14.2 us  [the longest x2 9.4 us: per_device(): jnp.dot(rows, flat_qkv, preferred_element_type=jnp.float32)]
    all_gather x2 -> x0, blocking collectives: 27.3 us -> none  [per_device(): lax.all_gather(normed, 'head', axis=0, tiled=True)]
    ppermute x2 -> x4, starting transfers between devices: 6.93 us -> 33.9 us  [the longest x1 15.8 us: per_device(): lax.ppermute(own, 'seq', [(i, (i + PLANE) % seq_count) for i in range(seq...]
    pallas_call x0 -> x2, Pallas kernels: none -> 25.9 us  [attend(): pl.pallas_call(attend_kernel, grid=(heads, keys // KEY_BLOCK), in_specs=[...]
    ppermute x2 -> x4, waiting for transfers between devices: 22 us -> 44.3 us  [the longest x1 24.9 us: per_device(): lax.ppermute(updated, ('segment', 'seq'), [(s * seq_count + q, (s + 1) %...]
    dynamic_slice x32 -> x0, local copies, waits for them, and re-layouts: 21.7 us -> none  [attend_piece(): lax.scan(step_block, running, (key_stack, value_stack, jnp.arange(blocks,...]
    reduce_sum x8 -> x0, other arithmetic: 19.9 us -> none  [attend_block(): row_sum = row_sum * rescale + jnp.sum(exponent, axis=2)]
  transfers between devices with their start and end apart: 8 -> 10, of which waited for: 8 -> 10; matrix products, arithmetic and copies ran while one was open for 0% -> 3% of each run, Pallas kernels for 0% -> 0%
where the time goes in v1:
time: 378 us; the launch traced here: 377 us
  waiting for transfers between devices  267 us (71%)
  starting transfers between devices  34.1 us (9%)
  Pallas kernels  25.9 us (7%)
  matrix products  14.2 us (4%)
  between operations  13.6 us (4%)
  local copies, waits for them, and re-layouts  10.8 us (3%)
  other arithmetic  10.6 us (3%)
    all_gather x2, waiting for transfers between devices, per_device(): lax.all_gather(projected[:, local_width:], 'seq', axis=0, tiled=True, axi...  91.4 us
    all_gather x2, waiting for transfers between devices, per_device(): rows = lax.all_gather(normed, 'head', axis=0, tiled=True)  69 us
    reduce_scatter x2, waiting for transfers between devices, per_device(): lax.psum_scatter(jnp.dot(attended, out_rows, preferred_element_type=jnp.f...  62.5 us
    pallas_call x2, Pallas kernels, attend(): pl.pallas_call(attend_kernel, grid=(heads, keys // KEY_BLOCK), in_specs=[...  25.9 us
    ppermute x1, waiting for transfers between devices, per_device(): lax.ppermute(updated, ('segment', 'seq'), [(s * seq_count + q, (s + 1) %...  24.9 us
    ppermute x1, starting transfers between devices, per_device(): lax.ppermute(own, 'seq', [(i, (i + PLANE) % seq_count) for i in range(seq...  15.8 us
    ppermute x2, waiting for transfers between devices, per_device(): lax.ppermute(updated, 'segment', [(i, (i + 1) % segment_count) for i in r...  14.8 us
    ppermute x1, starting transfers between devices, per_device(): lax.ppermute(updated, ('segment', 'seq'), [(s * seq_count + q, (s + 1) %...  12 us
  transfers between devices with their start and end apart: 10, of which 10 were waited for; matrix products, arithmetic and copies ran while one was open for 3% of the time, Pallas kernels for 0%

profile of v1, /device:TPU:8, one launch (start us, length us, event | category | flops | bytes accessed | tf_op | source)
XLA Modules:
  0.0 376.6 jit_solution(14155458942789159212)
XLA Ops:
  6.5 15.8 %collective-permute-start = (bf16[64,1536]{1,0:T(8,128)(2,1)}, bf16[64,1536]{1,0:T(8,128)(2,1)S(1)}, u32[]{:S(2)}, u32[]{:S(2)}) collective-permute-start(bf16[64,1536]{1,0:T(8,128)(2,1)} %bitcast.22), channel_id=1, source_target_pairs={{0,32},{4,36},{8,40},{12,44},{16,48},{20,52},{24,56},{28,60},{32,0... | collective-permute-start | bytes 589832 | tf_op jit(solution)/shard_map/ppermute | solution.py:94
  22.4 0.7 convert_element_type.50
  23.1 4.7 %collective-permute-done = bf16[64,1536]{1,0:T(8,128)(2,1)S(1)} collective-permute-done((bf16[64,1536]{1,0:T(8,128)(2,1)}, bf16[64,1536]{1,0:T(8,128)(2,1)S(1)}, u32[]{:S(2)}, u32[]{:S(2)}) %collective-permute-start) | collective-permute-done | bytes 196640 | tf_op jit(solution)/shard_map/ppermute | solution.py:94
  27.8 1.1 convert_reduce_fusion.1
  28.9 1.2 fusion.10
  30.1 1.9 fusion.13
  32.0 6.2 %copy.7 = bf16[1,1536,3,384]{1,3,2,0:T(8,128)(2,1)} copy(bf16[1,1536,3,384]{3,1,2,0:T(8,128)(2,1)} %param.10) | data formatting | bytes 7077888 | tf_op args[4]
  38.2 39.3 %all-gather.5.cloned.1.call-done = bf16[512,1536]{1,0:T(8,128)(2,1)} async-done(((bf16[128,1536]{1,0:T(8,128)(2,1)}), bf16[512,1536]{1,0:T(8,128)(2,1)}) %all-gather.5.cloned.1.call-update) | async-done | bytes 1572880 | tf_op jit(solution)/shard_map/all_gather | solution.py:102
  77.5 4.7 %convolution_convert_fusion.1 = bf16[512,1152]{1,0:T(8,128)(2,1)S(1)} fusion(bf16[512,1536]{1,0:T(8,128)(2,1)} %all-gather.5.cloned.1.call-done, bf16[1536,1152]{0,1:T(8,128)(2,1)} %bitcast.20), kind=kOutput, calls=%fused_computation.1 | convolution fusion | flops 1812529152 | bytes 6291456 | tf_op jit(solution)/shard_map/dot_general | solution.py:103
  82.2 0.9 slice.40
  83.9 1.2 pad_add_fusion.info_ref
  85.8 45.4 %all-gather.7.cloned.1.call-done.k_ref.v_ref = bf16[4096,768]{1,0:T(8,128)(2,1)} async-done(((bf16[512,768]{1,0:T(8,128)(2,1)}), bf16[4096,768]{1,0:T(8,128)(2,1)}) %all-gather.7.cloned.1.call-update) | async-done | bytes 6291472 | tf_op jit(solution)/shard_map/all_gather | solution.py:107
  131.1 13.0 %shard_map.64 = bf16[256,384]{1,0:T(8,128)(2,1)} custom-call(s32[2]{0:T(128)} %pad_add_fusion.info_ref, bf16[256,384]{1,0:T(8,128)(2,1)} %bitcast.28, bf16[4096,768]{1,0:T(8,128)(2,1)} %all-gather.7.cloned.1.call-done.k_ref.v_ref, bf16[4096,768]{1,0:T(8,128)(2,1)} %all-gather.7.cloned.1.call-done.k_ref.v_ref), custom_call_target="tpu_custom_call" | custom-call | tf_op jit(solution)/shard_map/pallas_call | solution.py:66
  144.1 2.4 convolution_convert_fusion.3
  146.7 31.2 %reduce-scatter.3.cloned.1.call-done = bf16[64,1536]{1,0:T(8,128)(2,1)} async-done(((bf16[256,1536]{1,0:T(8,128)(2,1)}), bf16[64,1536]{1,0:T(8,128)(2,1)}) %reduce-scatter.3.cloned.1.call-update) | async-done | bytes 196624 | tf_op jit(solution)/shard_map/reduce_scatter | solution.py:111
  177.9 1.0 add_convert_fusion.1
  178.8 12.0 %collective-permute-start.2 = (bf16[64,1536]{1,0:T(8,128)(2,1)S(1)}, bf16[64,1536]{1,0:T(8,128)(2,1)S(1)}, u32[]{:S(2)}, u32[]{:S(2)}) collective-permute-start(bf16[64,1536]{1,0:T(8,128)(2,1)S(1)} %add_convert_fusion.1), channel_id=1, source_target_pairs={{0,96},{4,100},{8,104},{12,108},{16,112},{20,116},{24,120},{28,124... | collective-permute-start | bytes 589832 | tf_op jit(solution)/shard_map/ppermute | solution.py:122
  190.9 2.6 collective-permute-start.1
  193.4 24.9 %collective-permute-done.2 = bf16[64,1536]{1,0:T(8,128)(2,1)S(1)} collective-permute-done((bf16[64,1536]{1,0:T(8,128)(2,1)S(1)}, bf16[64,1536]{1,0:T(8,128)(2,1)S(1)}, u32[]{:S(2)}, u32[]{:S(2)}) %collective-permute-start.2) | collective-permute-done | bytes 196640 | tf_op jit(solution)/shard_map/ppermute | solution.py:122
  218.3 3.8 %collective-permute-done.1 = bf16[64,1536]{1,0:T(8,128)(2,1)S(1)} collective-permute-done((bf16[64,1536]{1,0:T(8,128)(2,1)S(1)}, bf16[64,1536]{1,0:T(8,128)(2,1)S(1)}, u32[]{:S(2)}, u32[]{:S(2)}) %collective-permute-start.1) | collective-permute-done | bytes 196640 | tf_op jit(solution)/shard_map/ppermute | solution.py:118
  222.5 1.0 fusion.9
  223.6 29.7 %all-gather.9.cloned.1.call-done = bf16[512,1536]{1,0:T(8,128)(2,1)} async-done(((bf16[128,1536]{1,0:T(8,128)(2,1)}), bf16[512,1536]{1,0:T(8,128)(2,1)}) %all-gather.9.cloned.1.call-update) | async-done | bytes 1572880 | tf_op jit(solution)/shard_map/all_gather | solution.py:102
  253.3 4.7 %convolution_convert_fusion = bf16[512,1152]{1,0:T(8,128)(2,1)S(1)} fusion(bf16[512,1536]{1,0:T(8,128)(2,1)} %all-gather.9.cloned.1.call-done, bf16[1536,1152]{0,1:T(8,128)(2,1)} %bitcast.21), kind=kOutput, calls=%fused_computation | convolution fusion | flops 1812529152 | bytes 6291456 | tf_op jit(solution)/shard_map/dot_general | solution.py:103
  258.0 0.9 slice.43
  259.0 1.2 pad_add_fusion.1.info_ref
  260.9 46.1 %all-gather.11.cloned.1.call-done.k_ref.v_ref = bf16[4096,768]{1,0:T(8,128)(2,1)} async-done(((bf16[512,768]{1,0:T(8,128)(2,1)}), bf16[4096,768]{1,0:T(8,128)(2,1)}) %all-gather.11.cloned.1.call-update) | async-done | bytes 6291472 | tf_op jit(solution)/shard_map/all_gather | solution.py:107
  307.0 13.0 %shard_map.65 = bf16[256,384]{1,0:T(8,128)(2,1)} custom-call(s32[2]{0:T(128)} %pad_add_fusion.1.info_ref, bf16[256,384]{1,0:T(8,128)(2,1)} %bitcast.29, bf16[4096,768]{1,0:T(8,128)(2,1)} %all-gather.11.cloned.1.call-done.k_ref.v_ref, bf16[4096,768]{1,0:T(8,128)(2,1)} %all-gather.11.cloned.1.call-done.k_ref.v_ref), custom_call_target="tpu_custom_call" | custom-call | tf_op jit(solution)/shard_map/pallas_call | solution.py:66
  319.9 2.4 convolution_convert_fusion.2
  322.3 31.3 %reduce-scatter.5.cloned.1.call-done = bf16[64,1536]{1,0:T(8,128)(2,1)} async-done(((bf16[256,1536]{1,0:T(8,128)(2,1)}), bf16[64,1536]{1,0:T(8,128)(2,1)}) %reduce-scatter.5.cloned.1.call-update) | async-done | bytes 196624 | tf_op jit(solution)/shard_map/reduce_scatter | solution.py:111
  353.6 1.0 add_convert_fusion
  354.6 3.4 collective-permute-start.3
  358.1 11.0 %collective-permute-done.3 = bf16[64,1536]{1,0:T(8,128)(2,1)S(1)} collective-permute-done((bf16[64,1536]{1,0:T(8,128)(2,1)S(1)}, bf16[64,1536]{1,0:T(8,128)(2,1)S(1)}, u32[]{:S(2)}, u32[]{:S(2)}) %collective-permute-start.3) | collective-permute-done | bytes 196640 | tf_op jit(solution)/shard_map/ppermute | solution.py:118
  (34 shorter events, 3.6 us)
Async XLA Ops:
  6.5 137.6 %copy-start = (bf16[1,384,1536]{2,1,0:T(8,128)(2,1)S(1)}, bf16[1,384,1536]{2,1,0:T(8,128)(2,1)}, u32[]{:S(2)}) copy-start(bf16[1,384,1536]{2,1,0:T(8,128)(2,1)} %param.11) | copy-start | bytes 3538948
  6.5 70.9 %all-gather.5.cloned.1.call-start = ((), (), s32[]{:S(2)}) async-start(), calls=%async_computation.2 | async-start | bytes 1966080 | tf_op jit(solution)/shard_map/all_gather | solution.py:102
  6.5 21.2 %collective-permute-start = (bf16[64,1536]{1,0:T(8,128)(2,1)}, bf16[64,1536]{1,0:T(8,128)(2,1)S(1)}, u32[]{:S(2)}, u32[]{:S(2)}) collective-permute-start(bf16[64,1536]{1,0:T(8,128)(2,1)} %bitcast.22), channel_id=1, source_target_pairs={{0,32},{4,36},{8,40},{12,44},{16,48},{20,52},{24,56},{28,60},{32,0... | collective-permute-start | bytes 589832 | tf_op jit(solution)/shard_map/ppermute | solution.py:94
  32.0 99.2 %all-gather.7.cloned.1.call-start = ((), (), s32[]{:S(2)}) async-start(), calls=%async_computation.3 | async-start | bytes 7077888 | tf_op jit(solution)/shard_map/all_gather | solution.py:107
  82.2 1.1 copy-start.3
  83.2 94.7 %reduce-scatter.3.cloned.1.call-start = ((), (), s32[]{:S(2)}) async-start(), calls=%async_computation.4 | async-start | bytes 983040 | tf_op jit(solution)/shard_map/reduce_scatter | solution.py:111
  144.1 2.5 copy-start.2
  144.1 33.7 %copy-start.1 = (bf16[1,64,1536]{2,1,0:T(8,128)(2,1)S(1)}, bf16[1,64,1536]{2,1,0:T(8,128)(2,1)}, u32[]{:S(2)}) copy-start(bf16[1,64,1536]{2,1,0:T(8,128)(2,1)} %param.6) | copy-start | bytes 589828
  146.6 106.7 %all-gather.9.cloned.1.call-start = ((), (), s32[]{:S(2)}) async-start(), calls=%async_computation.5 | async-start | bytes 1966080 | tf_op jit(solution)/shard_map/all_gather | solution.py:102
  178.8 39.5 %collective-permute-start.2 = (bf16[64,1536]{1,0:T(8,128)(2,1)S(1)}, bf16[64,1536]{1,0:T(8,128)(2,1)S(1)}, u32[]{:S(2)}, u32[]{:S(2)}) collective-permute-start(bf16[64,1536]{1,0:T(8,128)(2,1)S(1)} %add_convert_fusion.1), channel_id=1, source_target_pairs={{0,96},{4,100},{8,104},{12,108},{16,112},{20,116},{24,120},{28,124... | collective-permute-start | bytes 589832 | tf_op jit(solution)/shard_map/ppermute | solution.py:122
  190.9 31.2 %collective-permute-start.1 = (bf16[64,1536]{1,0:T(8,128)(2,1)S(1)}, bf16[64,1536]{1,0:T(8,128)(2,1)S(1)}, u32[]{:S(2)}, u32[]{:S(2)}) collective-permute-start(bf16[64,1536]{1,0:T(8,128)(2,1)S(1)} %add_convert_fusion.1), channel_id=1, source_target_pairs={{0,64},{64,128},{128,192},{192,256},{256,320},{320,384},{384,448},... | collective-permute-start | bytes 589832 | tf_op jit(solution)/shard_map/ppermute | solution.py:118
  223.5 83.4 %all-gather.11.cloned.1.call-start = ((), (), s32[]{:S(2)}) async-start(), calls=%async_computation.6 | async-start | bytes 7077888 | tf_op jit(solution)/shard_map/all_gather | solution.py:107
  259.0 94.7 %reduce-scatter.5.cloned.1.call-start = ((), (), s32[]{:S(2)}) async-start(), calls=%async_computation.7 | async-start | bytes 983040 | tf_op jit(solution)/shard_map/reduce_scatter | solution.py:111
  354.6 14.4 %collective-permute-start.3 = (bf16[64,1536]{1,0:T(8,128)(2,1)S(1)}, bf16[64,1536]{1,0:T(8,128)(2,1)S(1)}, u32[]{:S(2)}, u32[]{:S(2)}) collective-permute-start(bf16[64,1536]{1,0:T(8,128)(2,1)S(1)} %add_convert_fusion), channel_id=1, source_target_pairs={{0,64},{64,128},{128,192},{192,256},{256,320},{320,384},{384,448},... | collective-permute-start | bytes 589832 | tf_op jit(solution)/shard_map/ppermute | solution.py:118
Sparse Core Ops, SparseCore 0:
  32.1 45.3 all-gather.4
  83.3 47.8 all-gather.6
  146.7 31.0 reduce-scatter.2
  223.7 29.6 all-gather.8
  259.1 47.8 all-gather.10
  322.5 31.1 reduce-scatter.4

commit v2 on v1

v2 whole, which is shorter than its diff:
```python
import math

import jax
import jax.numpy as jnp
from jax import lax
from jax.experimental import pallas as pl
from jax.experimental.pallas import tpu as pltpu
from jax.sharding import PartitionSpec as P

HEAD = 128
TICKS = 2
PLANE = 8
MESH = pl.DeviceIdType.MESH
EXP2_SCALE = HEAD ** (-0.5) * math.log2(math.e)


def layer_norm(values):
    row_mean = jnp.mean(values, axis=-1, keepdims=True)
    centered = values - row_mean
    row_var = jnp.mean(centered * centered, axis=-1, keepdims=True)
    return centered / jnp.sqrt(row_var + 1e-06)


def barrier(peers):
    sem = pltpu.get_barrier_semaphore()
    for peer in peers:
        pl.semaphore_signal(sem, inc=1, device_id=peer, device_id_type=MESH)
    pl.semaphore_wait(sem, len(peers))


def remote(src, dst, send_sem, recv_sem, index, peer):
    return pltpu.make_async_remote_copy(
        src_ref=src,
        dst_ref=dst,
        send_sem=send_sem.at[index],
        recv_sem=recv_sem.at[index],
        device_id=peer,
        device_id_type=MESH,
    )


def head_gather_kernel(block_ref, out_ref, send_sem, recv_sem, local_sem):
    me = lax.axis_index("head")
    right = lax.rem(me + 1, 4)
    left = lax.rem(me + 3, 4)
    rows = block_ref.shape[0]
    first, second = pl.ds(0, rows // 2), pl.ds(rows // 2, rows // 2)
    barrier([{"head": left}, {"head": right}])
    keep = pltpu.make_async_copy(block_ref, out_ref.at[me], local_sem)
    right_first = remote(block_ref.at[first], out_ref.at[me, first], send_sem, recv_sem, 0, {"head": right})
    left_second = remote(block_ref.at[second], out_ref.at[me, second], send_sem, recv_sem, 1, {"head": left})
    right_second = remote(block_ref.at[second], out_ref.at[me, second], send_sem, recv_sem, 2, {"head": right})
    left_first = remote(block_ref.at[first], out_ref.at[me, first], send_sem, recv_sem, 3, {"head": left})
    on_right = remote(out_ref.at[left, first], out_ref.at[left, first], send_sem, recv_sem, 4, {"head": right})
    on_left = remote(out_ref.at[right, second], out_ref.at[right, second], send_sem, recv_sem, 5, {"head": left})
    right_first.start()
    left_second.start()
    right_second.start()
    left_first.start()
    keep.start()
    right_first.wait_recv()
    on_right.start()
    left_second.wait_recv()
    on_left.start()
    right_second.wait_recv()
    left_first.wait_recv()
    on_right.wait_recv()
    on_left.wait_recv()
    keep.wait()
    for copy in (right_first, left_second, right_second, left_first, on_right, on_left):
        copy.wait_send()


def head_gather(block):
    rows, width = block.shape
    return pl.pallas_call(
        head_gather_kernel,
        out_shape=jax.ShapeDtypeStruct((4, rows, width), block.dtype),
        in_specs=[pl.BlockSpec(memory_space=pltpu.VMEM)],
        out_specs=pl.BlockSpec(memory_space=pltpu.VMEM),
        scratch_shapes=[
            pltpu.SemaphoreType.DMA((6,)),
            pltpu.SemaphoreType.DMA((6,)),
            pltpu.SemaphoreType.DMA,
        ],
        compiler_params=pltpu.CompilerParams(collective_id=0, has_side_effects=True),
    )(block)


def attend_kernel(length_ref, q_ref, kv_ref, o_ref, buf, max_ref, sum_ref, acc_ref, send_sem, recv_sem):
    seq = lax.axis_index("seq")
    half = lax.div(seq, PLANE)
    y = lax.rem(lax.div(seq, 2), 4)
    core = lax.rem(seq, 2)
    base = half * PLANE
    right = {"seq": base + lax.rem(y + 1, 4) * 2 + core}
    left = {"seq": base + lax.rem(y + 3, 4) * 2 + core}
    partner = {"seq": base + y * 2 + (1 - core)}
    rows = kv_ref.shape[0]
    heads = q_ref.shape[1] // HEAD
    first, second = pl.ds(0, rows // 2), pl.ds(rows // 2, rows // 2)
    length = length_ref[0]

    barrier([left, right, partner])
    right_first = remote(kv_ref.at[first], buf.at[3, 0, first], send_sem, recv_sem, 0, right)
    left_second = remote(kv_ref.at[second], buf.at[1, 0, second], send_sem, recv_sem, 1, left)
    right_second = remote(kv_ref.at[second], buf.at[3, 0, second], send_sem, recv_sem, 2, right)
    left_first = remote(kv_ref.at[first], buf.at[1, 0, first], send_sem, recv_sem, 3, left)
    across_own = remote(kv_ref, buf.at[0, 1], send_sem, recv_sem, 4, partner)
    on_right = remote(buf.at[3, 0, first], buf.at[2, 0, first], send_sem, recv_sem, 5, right)
    on_left = remote(buf.at[1, 0, second], buf.at[2, 0, second], send_sem, recv_sem, 6, left)
    across_left = remote(buf.at[3, 0], buf.at[3, 1], send_sem, recv_sem, 7, partner)
    across_right = remote(buf.at[1, 0], buf.at[1, 1], send_sem, recv_sem, 8, partner)
    across_first = remote(buf.at[2, 0, first], buf.at[2, 1, first], send_sem, recv_sem, 9, partner)
    across_second = remote(buf.at[2, 0, second], buf.at[2, 1, second], send_sem, recv_sem, 10, partner)

    def attend_shard(shard, distance, other_core):
        source = lax.rem(y + distance, 4) * 2 + lax.rem(core + other_core, 2)
        row = lax.broadcasted_iota(jnp.int32, (1, rows), 1)
        slot = jnp.bitwise_and(jnp.right_shift(row, 6), 1)
        which = jnp.bitwise_xor(slot, half)
        position = which * 2048 + source * 256 + jnp.right_shift(row, 7) * 64 + jnp.bitwise_and(row, 63)
        valid = position < length

        def one_head(h, carry):
            k_columns = pl.ds(pl.multiple_of(h * HEAD, HEAD), HEAD)
            v_columns = pl.ds(pl.multiple_of((heads + h) * HEAD, HEAD), HEAD)
            scores = lax.dot_general(
                q_ref[:, k_columns],
                shard[:, k_columns],
                (((1,), (1,)), ((), ())),
                preferred_element_type=jnp.float32,
            )
            scores = jnp.where(valid, scores * EXP2_SCALE, -1e30)
            old_max = max_ref[h]
            new_max = jnp.maximum(old_max, jnp.max(scores, axis=1, keepdims=True))
            rescale = jnp.exp2(old_max - new_max)
            weights = jnp.exp2(scores - new_max[:, :1])
            max_ref[h] = new_max
            sum_ref[h] = sum_ref[h] * rescale + jnp.sum(weights, axis=1, keepdims=True)
            acc_ref[h] = acc_ref[h] * rescale + jnp.dot(
                weights.astype(jnp.bfloat16), shard[:, v_columns], preferred_element_type=jnp.float32
            )
            return carry

        lax.fori_loop(0, heads, one_head, 0)

    right_first.start()
    left_second.start()
    right_second.start()
    left_first.start()
    across_own.start()
    max_ref[...] = jnp.full_like(max_ref, -1e30)
    sum_ref[...] = jnp.zeros_like(sum_ref)
    acc_ref[...] = jnp.zeros_like(acc_ref)
    attend_shard(kv_ref, 0, 0)
    right_first.wait_recv()
    on_right.start()
    left_second.wait_recv()
    on_left.start()
    across_own.wait_recv()
    attend_shard(buf.at[0, 1], 0, 1)
    right_second.wait_recv()
    across_left.start()
    left_first.wait_recv()
    across_right.start()
    attend_shard(buf.at[3, 0], 3, 0)
    attend_shard(buf.at[1, 0], 1, 0)
    on_right.wait_recv()
    across_first.start()
    on_left.wait_recv()
    across_second.start()
    across_left.wait_recv()
    attend_shard(buf.at[3, 1], 3, 1)
    across_right.wait_recv()
    attend_shard(buf.at[1, 1], 1, 1)
    attend_shard(buf.at[2, 0], 2, 0)
    across_first.wait_recv()
    across_second.wait_recv()
    attend_shard(buf.at[2, 1], 2, 1)
    for h in range(heads):
        o_ref[:, h * HEAD : (h + 1) * HEAD] = (acc_ref[h] / sum_ref[h]).astype(o_ref.dtype)
    for copy in (
        right_first,
        left_second,
        right_second,
        left_first,
        across_own,
        on_right,
        on_left,
        across_left,
        across_right,
        across_first,
        across_second,
    ):
        copy.wait_send()


def attend(length, queries, key_value):
    rows, width = queries.shape
    heads = width // HEAD
    stats = pltpu.VMEM((heads, rows, HEAD), jnp.float32)
    return pl.pallas_call(
        attend_kernel,
        in_specs=[
            pl.BlockSpec(memory_space=pltpu.SMEM),
            pl.BlockSpec(memory_space=pltpu.VMEM),
            pl.BlockSpec(memory_space=pltpu.VMEM),
        ],
        out_specs=pl.BlockSpec(memory_space=pltpu.VMEM),
        out_shape=jax.ShapeDtypeStruct((rows, width), jnp.bfloat16),
        scratch_shapes=[
            pltpu.VMEM((4, 2) + key_value.shape, key_value.dtype),
            stats,
            stats,
            stats,
            pltpu.SemaphoreType.DMA((11,)),
            pltpu.SemaphoreType.DMA((11,)),
        ],
        compiler_params=pltpu.CompilerParams(collective_id=1, has_side_effects=True),
    )(length, queries, key_value)


def per_device(tokens, lengths, modulation, gate_gain, w_qkv, w_out):
    segment_count = lax.axis_size("segment")
    seq_count = lax.axis_size("seq")
    position = lax.axis_index("segment")
    shift_scale = modulation[0].astype(jnp.float32)
    gate_row = gate_gain[0].astype(jnp.float32)
    model_width = w_qkv.shape[1]
    local_width = w_qkv.shape[3]
    flat_qkv = w_qkv[0].reshape(model_width, 3 * local_width)
    out_rows = w_out[0]
    own = tokens[0]
    other = lax.ppermute(own, "seq", [(i, (i + PLANE) % seq_count) for i in range(seq_count)])
    for tick_index in range(TICKS):
        micro_index = (position - tick_index) % segment_count
        length = lax.dynamic_index_in_dim(lengths, micro_index, 0, keepdims=False)
        values = own.astype(jnp.float32)
        both = jnp.concatenate([own, other], axis=0).astype(jnp.float32)
        normed = (layer_norm(both) * (1.0 + shift_scale[1]) + shift_scale[0]).astype(jnp.bfloat16)
        rows = head_gather(normed).reshape(-1, model_width)
        projected = jnp.dot(rows, flat_qkv, preferred_element_type=jnp.float32).astype(jnp.bfloat16)
        tile = own.shape[0]
        queries = projected[:, :local_width].reshape(-1, 2, tile, local_width)[:, 0]
        queries = queries.reshape(-1, local_width)
        attended = attend(length[None], queries, projected[:, local_width:])
        branch = lax.psum_scatter(
            jnp.dot(attended, out_rows, preferred_element_type=jnp.float32).astype(jnp.bfloat16),
            "head",
            scatter_dimension=0,
            tiled=True,
        ).astype(jnp.float32)
        updated = (values + gate_row * branch).astype(jnp.bfloat16)
        own = lax.ppermute(
            updated, "segment", [(i, (i + 1) % segment_count) for i in range(segment_count)]
        )
        if tick_index + 1 < TICKS:
            other = lax.ppermute(
                updated,
                ("segment", "seq"),
                [
                    (s * seq_count + q, (s + 1) % segment_count * seq_count + (q + PLANE) % seq_count)
                    for s in range(segment_count)
                    for q in range(seq_count)
                ],
            )
    return own[None]


def solution(mesh):
    return jax.shard_map(
        per_device,
        mesh=mesh,
        in_specs=(
            P("segment", ("seq", "head"), None),
            P(),
            P("segment", None, None),
            P("segment", None),
            P("segment", None, None, "head"),
            P("segment", "head", None),
        ),
        out_specs=P("segment", ("seq", "head"), None),
        check_vma=False,
    )
```

time: 378 us -> 297 us (0.79)
  waiting for transfers between devices: 267 us -> 102 us
  Pallas kernels: 25.9 us -> 116 us
  other arithmetic: 10.6 us -> 5.54 us
    all_gather x4 -> x0, waiting for transfers between devices: 160 us -> none  [the longest x2 91.4 us: per_device(): lax.all_gather(projected[:, local_width:], 'seq', axis=0, tiled=True, axi...]
    pallas_call x2 -> x4, Pallas kernels: 25.9 us -> 116 us  [the longest x2 77.5 us: attend(): pl.pallas_call(attend_kernel, in_specs=[pl.BlockSpec(memory_space=pltpu.S...]
    ppermute x1, waiting for transfers between devices: 4.66 us -> 0.01 us  [per_device(): lax.ppermute(own, 'seq', [(i, (i + PLANE) % seq_count) for i in range(seq...]
  transfers between devices with their start and end apart: 10 -> 6, of which waited for: 10 -> 5; matrix products, arithmetic and copies ran while one was open for 3% -> 3% of each run, Pallas kernels for 0% -> 0%
where the time goes in v2:
time: 297 us
  Pallas kernels  116 us (39%)
  waiting for transfers between devices  102 us (34%)
  starting transfers between devices  34.2 us (12%)
  matrix products  14.2 us (5%)
  between operations  13.6 us (5%)
  local copies, waits for them, and re-layouts  10.8 us (4%)
  other arithmetic  5.54 us (2%)
    pallas_call x2, Pallas kernels, attend(): pl.pallas_call(attend_kernel, in_specs=[pl.BlockSpec(memory_space=pltpu.S...  77.5 us
    reduce_scatter x2, waiting for transfers between devices, per_device(): lax.psum_scatter(jnp.dot(attended, out_rows, preferred_element_type=jnp.f...  62.5 us
    pallas_call x2, Pallas kernels, head_gather(): pl.pallas_call(head_gather_kernel, out_shape=jax.ShapeDtypeStruct((4, row...  38.7 us
    ppermute x1, waiting for transfers between devices, per_device(): lax.ppermute(updated, ('segment', 'seq'), [(s * seq_count + q, (s + 1) %...  24.7 us
    ppermute x1, starting transfers between devices, per_device(): lax.ppermute(own, 'seq', [(i, (i + PLANE) % seq_count) for i in range(seq...  15.8 us
    ppermute x2, waiting for transfers between devices, per_device(): lax.ppermute(updated, 'segment', [(i, (i + 1) % segment_count) for i in r...  14.8 us
    ppermute x1, starting transfers between devices, per_device(): lax.ppermute(updated, ('segment', 'seq'), [(s * seq_count + q, (s + 1) %...  12 us
    dot_general x2, matrix products, per_device(): jnp.dot(rows, flat_qkv, preferred_element_type=jnp.float32)  9.4 us
  transfers between devices with their start and end apart: 6, of which 5 were waited for; matrix products, arithmetic and copies ran while one was open for 3% of the time, Pallas kernels for 0%

profile of v2, /device:TPU:8, one launch (start us, length us, event | category | flops | bytes accessed | tf_op | source)
XLA Modules:
  0.0 296.6 jit_solution(17122918962486772349)
XLA Ops:
  6.5 15.8 %collective-permute-start = (bf16[64,1536]{1,0:T(8,128)(2,1)}, bf16[64,1536]{1,0:T(8,128)(2,1)S(1)}, u32[]{:S(2)}, u32[]{:S(2)}) collective-permute-start(bf16[64,1536]{1,0:T(8,128)(2,1)} %bitcast.23), channel_id=1, source_target_pairs={{0,32},{4,36},{8,40},{12,44},{16,48},{20,52},{24,56},{28,60},{32,0... | collective-permute-start | bytes 589832 | tf_op jit(solution)/shard_map/ppermute | solution.py:235
  22.4 0.7 convert_element_type.50
  23.1 6.1 %copy.7 = bf16[1,1536,3,384]{1,3,2,0:T(8,128)(2,1)} copy(bf16[1,1536,3,384]{3,1,2,0:T(8,128)(2,1)} %param.10) | data formatting | bytes 7077888 | tf_op args[4]
  29.3 0.7 fusion.15
  30.0 0.1 convert_reduce_fusion.1
  30.1 0.3 fusion.10
  30.4 1.0 fusion.13.block_ref
  31.4 19.3 %shard_map.64 = bf16[4,128,1536]{2,1,0:T(8,128)(2,1)} custom-call(bf16[128,1536]{1,0:T(8,128)(2,1)} %fusion.13.block_ref), custom_call_target="tpu_custom_call" | custom-call | tf_op jit(solution)/shard_map/pallas_call | solution.py:76
  50.7 4.7 %convolution_convert_fusion.1 = bf16[512,1152]{1,0:T(8,128)(2,1)S(1)} fusion(bf16[512,1536]{1,0:T(8,128)(2,1)} %bitcast.28, bf16[1536,1152]{0,1:T(8,128)(2,1)} %bitcast.21), kind=kOutput, calls=%fused_computation.1 | convolution fusion | flops 1812529152 | bytes 6291456 | tf_op jit(solution)/shard_map/dot_general | solution.py:243
  55.5 0.9 slice.40.kv_ref
  56.4 0.7 slice.39
  57.1 38.8 %shard_map.65 = bf16[256,384]{1,0:T(8,128)(2,1)} custom-call(s32[1]{0:T(128)} %get-tuple-element.7.length_ref, bf16[256,384]{1,0:T(8,128)(2,1)} %bitcast.32, bf16[512,768]{1,0:T(8,128)(2,1)} %slice.40.kv_ref), custom_call_target="tpu_custom_call" | custom-call | tf_op jit(solution)/shard_map/pallas_call | solution.py:203
  95.9 2.4 convolution_convert_fusion.3
  98.4 37.2 %reduce-scatter.3.cloned.1.call-done = bf16[64,1536]{1,0:T(8,128)(2,1)} async-done(((bf16[256,1536]{1,0:T(8,128)(2,1)}), bf16[64,1536]{1,0:T(8,128)(2,1)}) %reduce-scatter.3.cloned.1.call-update) | async-done | bytes 196624 | tf_op jit(solution)/shard_map/reduce_scatter | solution.py:248
  135.6 1.0 add_convert_fusion.1
  136.6 12.0 %collective-permute-start.2 = (bf16[64,1536]{1,0:T(8,128)(2,1)S(1)}, bf16[64,1536]{1,0:T(8,128)(2,1)S(1)}, u32[]{:S(2)}, u32[]{:S(2)}) collective-permute-start(bf16[64,1536]{1,0:T(8,128)(2,1)S(1)} %add_convert_fusion.1), channel_id=1, source_target_pairs={{0,96},{4,100},{8,104},{12,108},{16,112},{20,116},{24,120},{28,124... | collective-permute-start | bytes 589832 | tf_op jit(solution)/shard_map/ppermute | solution.py:259
  148.6 2.8 collective-permute-start.1
  151.4 24.7 %collective-permute-done.2 = bf16[64,1536]{1,0:T(8,128)(2,1)S(1)} collective-permute-done((bf16[64,1536]{1,0:T(8,128)(2,1)S(1)}, bf16[64,1536]{1,0:T(8,128)(2,1)S(1)}, u32[]{:S(2)}, u32[]{:S(2)}) %collective-permute-start.2) | collective-permute-done | bytes 196640 | tf_op jit(solution)/shard_map/ppermute | solution.py:259
  176.1 3.8 %collective-permute-done.1 = bf16[64,1536]{1,0:T(8,128)(2,1)S(1)} collective-permute-done((bf16[64,1536]{1,0:T(8,128)(2,1)S(1)}, bf16[64,1536]{1,0:T(8,128)(2,1)S(1)}, u32[]{:S(2)}, u32[]{:S(2)}) %collective-permute-start.1) | collective-permute-done | bytes 196640 | tf_op jit(solution)/shard_map/ppermute | solution.py:255
  180.1 0.3 fusion.6
  180.4 1.0 fusion.9.block_ref
  181.4 19.4 %shard_map.66 = bf16[4,128,1536]{2,1,0:T(8,128)(2,1)} custom-call(bf16[128,1536]{1,0:T(8,128)(2,1)} %fusion.9.block_ref), custom_call_target="tpu_custom_call" | custom-call | tf_op jit(solution)/shard_map/pallas_call | solution.py:76
  200.8 4.7 %convolution_convert_fusion = bf16[512,1152]{1,0:T(8,128)(2,1)S(1)} fusion(bf16[512,1536]{1,0:T(8,128)(2,1)} %bitcast.27, bf16[1536,1152]{0,1:T(8,128)(2,1)} %bitcast.22), kind=kOutput, calls=%fused_computation | convolution fusion | flops 1812529152 | bytes 6291456 | tf_op jit(solution)/shard_map/dot_general | solution.py:243
  205.5 0.9 slice.43.kv_ref
  206.5 0.7 slice.42
  207.2 38.7 %shard_map.67 = bf16[256,384]{1,0:T(8,128)(2,1)} custom-call(s32[1]{0:T(128)} %get-tuple-element.8.length_ref, bf16[256,384]{1,0:T(8,128)(2,1)} %bitcast.31, bf16[512,768]{1,0:T(8,128)(2,1)} %slice.43.kv_ref), custom_call_target="tpu_custom_call" | custom-call | tf_op jit(solution)/shard_map/pallas_call | solution.py:203
  245.9 2.4 convolution_convert_fusion.2
  248.3 25.3 %reduce-scatter.5.cloned.1.call-done = bf16[64,1536]{1,0:T(8,128)(2,1)} async-done(((bf16[256,1536]{1,0:T(8,128)(2,1)}), bf16[64,1536]{1,0:T(8,128)(2,1)}) %reduce-scatter.5.cloned.1.call-update) | async-done | bytes 196624 | tf_op jit(solution)/shard_map/reduce_scatter | solution.py:248
  273.6 1.0 add_convert_fusion
  274.6 3.5 %collective-permute-start.3 = (bf16[64,1536]{1,0:T(8,128)(2,1)S(1)}, bf16[64,1536]{1,0:T(8,128)(2,1)S(1)}, u32[]{:S(2)}, u32[]{:S(2)}) collective-permute-start(bf16[64,1536]{1,0:T(8,128)(2,1)S(1)} %add_convert_fusion), channel_id=1, source_target_pairs={{0,64},{64,128},{128,192},{192,256},{256,320},{320,384},{384,448},... | collective-permute-start | bytes 589832 | tf_op jit(solution)/shard_map/ppermute | solution.py:255
  278.1 10.9 %collective-permute-done.3 = bf16[64,1536]{1,0:T(8,128)(2,1)S(1)} collective-permute-done((bf16[64,1536]{1,0:T(8,128)(2,1)S(1)}, bf16[64,1536]{1,0:T(8,128)(2,1)S(1)}, u32[]{:S(2)}, u32[]{:S(2)}) %collective-permute-start.3) | collective-permute-done | bytes 196640 | tf_op jit(solution)/shard_map/ppermute | solution.py:255
  289.0 0.7 copy.9
  (22 shorter events, 0.4 us)
Async XLA Ops:
  6.5 89.4 %copy-start = (bf16[1,384,1536]{2,1,0:T(8,128)(2,1)S(1)}, bf16[1,384,1536]{2,1,0:T(8,128)(2,1)}, u32[]{:S(2)}) copy-start(bf16[1,384,1536]{2,1,0:T(8,128)(2,1)} %param.11) | copy-start | bytes 3538948
  6.5 129.1 %reduce-scatter.3.cloned.1.call-start = ((), (), s32[]{:S(2)}) async-start(), calls=%async_computation.2 | async-start | bytes 983040 | tf_op jit(solution)/shard_map/reduce_scatter | solution.py:248
  6.5 23.4 %collective-permute-start = (bf16[64,1536]{1,0:T(8,128)(2,1)}, bf16[64,1536]{1,0:T(8,128)(2,1)S(1)}, u32[]{:S(2)}, u32[]{:S(2)}) collective-permute-start(bf16[64,1536]{1,0:T(8,128)(2,1)} %bitcast.23), channel_id=1, source_target_pairs={{0,32},{4,36},{8,40},{12,44},{16,48},{20,52},{24,56},{28,60},{32,0... | collective-permute-start | bytes 589832 | tf_op jit(solution)/shard_map/ppermute | solution.py:235
  23.1 6.1 %copy-start.3 = (s32[8]{0:T(128)S(1)}, s32[8]{0:T(128)}, u32[]{:S(2)}) copy-start(s32[8]{0:T(128)} %param.7) | copy-start | bytes 100
  23.1 6.8 %copy-start.1 = (bf16[1,64,1536]{2,1,0:T(8,128)(2,1)S(1)}, bf16[1,64,1536]{2,1,0:T(8,128)(2,1)}, u32[]{:S(2)}) copy-start(bf16[1,64,1536]{2,1,0:T(8,128)(2,1)} %param.6) | copy-start | bytes 589828
  95.9 2.5 copy-start.2
  98.3 175.3 %reduce-scatter.5.cloned.1.call-start = ((), (), s32[]{:S(2)}) async-start(), calls=%async_computation.3 | async-start | bytes 983040 | tf_op jit(solution)/shard_map/reduce_scatter | solution.py:248
  136.6 39.5 %collective-permute-start.2 = (bf16[64,1536]{1,0:T(8,128)(2,1)S(1)}, bf16[64,1536]{1,0:T(8,128)(2,1)S(1)}, u32[]{:S(2)}, u32[]{:S(2)}) collective-permute-start(bf16[64,1536]{1,0:T(8,128)(2,1)S(1)} %add_convert_fusion.1), channel_id=1, source_target_pairs={{0,96},{4,100},{8,104},{12,108},{16,112},{20,116},{24,120},{28,124... | collective-permute-start | bytes 589832 | tf_op jit(solution)/shard_map/ppermute | solution.py:259
  148.6 31.3 %collective-permute-start.1 = (bf16[64,1536]{1,0:T(8,128)(2,1)S(1)}, bf16[64,1536]{1,0:T(8,128)(2,1)S(1)}, u32[]{:S(2)}, u32[]{:S(2)}) collective-permute-start(bf16[64,1536]{1,0:T(8,128)(2,1)S(1)} %add_convert_fusion.1), channel_id=1, source_target_pairs={{0,64},{64,128},{128,192},{192,256},{256,320},{320,384},{384,448},... | collective-permute-start | bytes 589832 | tf_op jit(solution)/shard_map/ppermute | solution.py:255
  274.6 14.5 %collective-permute-start.3 = (bf16[64,1536]{1,0:T(8,128)(2,1)S(1)}, bf16[64,1536]{1,0:T(8,128)(2,1)S(1)}, u32[]{:S(2)}, u32[]{:S(2)}) collective-permute-start(bf16[64,1536]{1,0:T(8,128)(2,1)S(1)} %add_convert_fusion), channel_id=1, source_target_pairs={{0,64},{64,128},{128,192},{192,256},{256,320},{320,384},{384,448},... | collective-permute-start | bytes 589832 | tf_op jit(solution)/shard_map/ppermute | solution.py:255
Sparse Core Ops, SparseCore 0:
  98.5 37.1 reduce-scatter.2
  248.4 25.1 reduce-scatter.4

commit v3 on v2

--- a/solution.py
+++ b/solution.py
@@ -221,6 +221,52 @@
     )(length, queries, key_value)
 
 
+def finish_kernel(partial_ref, state_ref, gate_ref, out_ref, landed, updated, send_sem, recv_sem):
+    me = lax.axis_index("head")
+    position = lax.axis_index("segment")
+    rows = state_ref.shape[0]
+    ahead = [lax.rem(me + distance, 4) for distance in (1, 2, 3)]
+    following = {"segment": lax.rem(position + 1, 8)}
+    preceding = {"segment": lax.rem(position + 7, 8)}
+    barrier([{"head": peer} for peer in ahead] + [preceding])
+    copies = []
+    for index in (1, 0, 2):
+        piece = pl.ds(pl.multiple_of(ahead[index] * rows, rows), rows)
+        copies.append(
+            remote(partial_ref.at[piece], landed.at[index], send_sem, recv_sem, index, {"head": ahead[index]})
+        )
+        copies[-1].start()
+    for copy in copies:
+        copy.wait_recv()
+    mine = pl.ds(pl.multiple_of(me * rows, rows), rows)
+    branch = partial_ref[mine, :].astype(jnp.float32)
+    for index in range(3):
+        branch = branch + landed[index].astype(jnp.float32)
+    updated[...] = (state_ref[...].astype(jnp.float32) + gate_ref[...] * branch).astype(updated.dtype)
+    onward = remote(updated, out_ref, send_sem, recv_sem, 3, following)
+    onward.start()
+    for copy in copies:
+        copy.wait_send()
+    onward.wait()
+
+
+def finish(partial, state, gate_row):
+    vmem = pl.BlockSpec(memory_space=pltpu.VMEM)
+    return pl.pallas_call(
+        finish_kernel,
+        in_specs=[vmem, vmem, vmem],
+        out_specs=vmem,
+        out_shape=jax.ShapeDtypeStruct(state.shape, state.dtype),
+        scratch_shapes=[
+            pltpu.VMEM((3,) + state.shape, partial.dtype),
+            pltpu.VMEM(state.shape, state.dtype),
+            pltpu.SemaphoreType.DMA((4,)),
+            pltpu.SemaphoreType.DMA((4,)),
+        ],
+        compiler_params=pltpu.CompilerParams(collective_id=2, has_side_effects=True),
+    )(partial, state, gate_row)
+
+
 def per_device(tokens, lengths, modulation, gate_gain, w_qkv, w_out):
     segment_count = lax.axis_size("segment")
     seq_count = lax.axis_size("seq")
@@ -232,11 +278,10 @@
     flat_qkv = w_qkv[0].reshape(model_width, 3 * local_width)
     out_rows = w_out[0]
     own = tokens[0]
-    other = lax.ppermute(own, "seq", [(i, (i + PLANE) % seq_count) for i in range(seq_count)])
     for tick_index in range(TICKS):
         micro_index = (position - tick_index) % segment_count
         length = lax.dynamic_index_in_dim(lengths, micro_index, 0, keepdims=False)
-        values = own.astype(jnp.float32)
+        other = lax.ppermute(own, "seq", [(i, (i + PLANE) % seq_count) for i in range(seq_count)])
         both = jnp.concatenate([own, other], axis=0).astype(jnp.float32)
         normed = (layer_norm(both) * (1.0 + shift_scale[1]) + shift_scale[0]).astype(jnp.bfloat16)
         rows = head_gather(normed).reshape(-1, model_width)
@@ -245,26 +290,8 @@
         queries = projected[:, :local_width].reshape(-1, 2, tile, local_width)[:, 0]
         queries = queries.reshape(-1, local_width)
         attended = attend(length[None], queries, projected[:, local_width:])
-        branch = lax.psum_scatter(
-            jnp.dot(attended, out_rows, preferred_element_type=jnp.float32).astype(jnp.bfloat16),
-            "head",
-            scatter_dimension=0,
-            tiled=True,
-        ).astype(jnp.float32)
-        updated = (values + gate_row * branch).astype(jnp.bfloat16)
-        own = lax.ppermute(
-            updated, "segment", [(i, (i + 1) % segment_count) for i in range(segment_count)]
-        )
-        if tick_index + 1 < TICKS:
-            other = lax.ppermute(
-                updated,
-                ("segment", "seq"),
-                [
-                    (s * seq_count + q, (s + 1) % segment_count * seq_count + (q + PLANE) % seq_count)
-                    for s in range(segment_count)
-                    for q in range(seq_count)
-                ],
-            )
+        partial = jnp.dot(attended, out_rows, preferred_element_type=jnp.float32).astype(jnp.bfloat16)
+        own = finish(partial, own, gate_row[None])
     return own[None]
 
 

time: 297 us -> 252 us (0.85)
  waiting for transfers between devices: 102 us -> 12 us
  Pallas kernels: 116 us -> 176 us
  between operations: 13.6 us -> 0.17 us
  starting transfers between devices: 34.2 us -> 29.1 us
    reduce_scatter x2 -> x0, waiting for transfers between devices: 62.5 us -> none  [per_device(): lax.psum_scatter(jnp.dot(attended, out_rows, preferred_element_type=jnp.f...]
    pallas_call x0 -> x2, Pallas kernels: none -> 60 us  [finish(): pl.pallas_call(finish_kernel, in_specs=[vmem, vmem, vmem], out_specs=vmem...]
    ppermute x3 -> x0, waiting for transfers between devices: 39.5 us -> none  [the longest x1 24.7 us: per_device(): lax.ppermute(updated, ('segment', 'seq'), [(s * seq_count + q, (s + 1) %...]
    ppermute x3 -> x0, starting transfers between devices: 18.3 us -> none  [the longest x1 12 us: per_device(): lax.ppermute(updated, ('segment', 'seq'), [(s * seq_count + q, (s + 1) %...]
    ppermute x1 -> x2, starting transfers between devices: 15.8 us -> 29.1 us  [per_device(): lax.ppermute(own, 'seq', [(i, (i + PLANE) % seq_count) for i in range(seq...]
    ppermute x1 -> x2, waiting for transfers between devices: 0.01 us -> 12 us  [per_device(): lax.ppermute(own, 'seq', [(i, (i + PLANE) % seq_count) for i in range(seq...]
    unnamed x10 -> x8, local copies, waits for them, and re-layouts: 6.81 us -> 7.75 us
  transfers between devices with their start and end apart: 6 -> 2, of which waited for: 5 -> 1; matrix products, arithmetic and copies ran while one was open for 3% -> 4% of each run, Pallas kernels for 0% -> 0%
where the time goes in v3:
time: 252 us; the launch traced here: 251 us
  Pallas kernels  176 us (70%)
  starting transfers between devices  29.1 us (12%)
  matrix products  14.2 us (6%)
  waiting for transfers between devices  12 us (5%)
  local copies, waits for them, and re-layouts  11.7 us (5%)
  other arithmetic  7.6 us (3%)
    pallas_call x2, Pallas kernels, attend(): pl.pallas_call(attend_kernel, in_specs=[pl.BlockSpec(memory_space=pltpu.S...  79.2 us
    pallas_call x2, Pallas kernels, finish(): pl.pallas_call(finish_kernel, in_specs=[vmem, vmem, vmem], out_specs=vmem...  60 us
    pallas_call x2, Pallas kernels, head_gather(): pl.pallas_call(head_gather_kernel, out_shape=jax.ShapeDtypeStruct((4, row...  37.2 us
    ppermute x2, starting transfers between devices, per_device(): lax.ppermute(own, 'seq', [(i, (i + PLANE) % seq_count) for i in range(seq...  29.1 us
    ppermute x2, waiting for transfers between devices, per_device(): lax.ppermute(own, 'seq', [(i, (i + PLANE) % seq_count) for i in range(seq...  12 us
    dot_general x2, matrix products, per_device(): jnp.dot(rows, flat_qkv, preferred_element_type=jnp.float32)  9.41 us
    unnamed x8, local copies, waits for them, and re-layouts  7.75 us
  transfers between devices with their start and end apart: 2, of which 1 were waited for; matrix products, arithmetic and copies ran while one was open for 4% of the time, Pallas kernels for 0%

profile of v3, /device:TPU:8, one launch (start us, length us, event | category | flops | bytes accessed | tf_op | source)
XLA Modules:
  0.0 251.2 jit_solution(12864360160177628352)
XLA Ops:
  0.0 0.0 copy-start
  0.0 15.8 %collective-permute-start = (bf16[64,1536]{1,0:T(8,128)(2,1)}, bf16[64,1536]{1,0:T(8,128)(2,1)S(1)}, u32[]{:S(2)}, u32[]{:S(2)}) collective-permute-start(bf16[64,1536]{1,0:T(8,128)(2,1)} %bitcast.22), channel_id=1, source_target_pairs={{0,32},{4,36},{8,40},{12,44},{16,48},{20,52},{24,56},{28,60},{32,0... | collective-permute-start | bytes 589832 | tf_op jit(solution)/shard_map/ppermute | solution.py:284
  15.9 1.3 convert_element_type.37.gate_ref
  17.2 0.7 convert_element_type.33
  17.9 6.1 %copy.7 = bf16[1,1536,3,384]{1,3,2,0:T(8,128)(2,1)} copy(bf16[1,1536,3,384]{3,1,2,0:T(8,128)(2,1)} %param.10) | data formatting | bytes 7077888 | tf_op args[4]
  24.0 0.0 copy-done.2
  24.0 0.7 fusion.15
  24.7 0.0 collective-permute-done
  24.7 0.1 convert_reduce_fusion.1
  24.9 0.3 fusion.10
  25.1 1.0 fusion.13.block_ref
  26.1 19.3 %shard_map.64 = bf16[4,128,1536]{2,1,0:T(8,128)(2,1)} custom-call(bf16[128,1536]{1,0:T(8,128)(2,1)} %fusion.13.block_ref), custom_call_target="tpu_custom_call" | custom-call | tf_op jit(solution)/shard_map/pallas_call | solution.py:76
  45.5 4.7 %convolution_convert_fusion.1 = bf16[512,1152]{1,0:T(8,128)(2,1)S(1)} fusion(bf16[512,1536]{1,0:T(8,128)(2,1)} %bitcast.28, bf16[1536,1152]{0,1:T(8,128)(2,1)} %bitcast.20), kind=kOutput, calls=%fused_computation.1 | convolution fusion | flops 1812529152 | bytes 6291456 | tf_op jit(solution)/shard_map/dot_general | solution.py:288
  50.2 0.9 slice.40.kv_ref
  51.2 0.7 slice.39
  51.9 38.7 %shard_map.65 = bf16[256,384]{1,0:T(8,128)(2,1)} custom-call(s32[1]{0:T(128)} %get-tuple-element.7.length_ref, bf16[256,384]{1,0:T(8,128)(2,1)} %bitcast.33, bf16[512,768]{1,0:T(8,128)(2,1)} %slice.40.kv_ref), custom_call_target="tpu_custom_call" | custom-call | tf_op jit(solution)/shard_map/pallas_call | solution.py:203
  90.5 0.0 copy-done
  90.5 2.4 convolution_convert_fusion.3.partial_ref
  92.9 28.6 %shard_map.66.state_ref = bf16[64,1536]{1,0:T(8,128)(2,1)} custom-call(bf16[256,1536]{1,0:T(8,128)(2,1)} %convolution_convert_fusion.3.partial_ref, bf16[64,1536]{1,0:T(8,128)(2,1)} %bitcast.23, f32[1,1536]{1,0:T(1,128)} %convert_element_type.37.gate_ref), custom_call_target="tpu_custom_call" | custom-call | tf_op jit(solution)/shard_map/pallas_call | solution.py:255
  121.6 13.3 %collective-permute-start.1 = (bf16[64,1536]{1,0:T(8,128)(2,1)}, bf16[64,1536]{1,0:T(8,128)(2,1)S(1)}, u32[]{:S(2)}, u32[]{:S(2)}) collective-permute-start(bf16[64,1536]{1,0:T(8,128)(2,1)} %shard_map.66.state_ref), channel_id=1, source_target_pairs={{0,32},{4,36},{8,40},{12,44},{16,48},{20,52},{24,56},{28,60},{32,0... | collective-permute-start | bytes 589832 | tf_op jit(solution)/shard_map/ppermute | solution.py:284
  134.8 12.0 %collective-permute-done.1 = bf16[64,1536]{1,0:T(8,128)(2,1)S(1)} collective-permute-done((bf16[64,1536]{1,0:T(8,128)(2,1)}, bf16[64,1536]{1,0:T(8,128)(2,1)S(1)}, u32[]{:S(2)}, u32[]{:S(2)}) %collective-permute-start.1) | collective-permute-done | bytes 196640 | tf_op jit(solution)/shard_map/ppermute | solution.py:284
  146.9 1.1 convert_reduce_fusion
  147.9 1.2 fusion.6
  149.1 1.9 fusion.9.block_ref
  151.0 17.9 %shard_map.67 = bf16[4,128,1536]{2,1,0:T(8,128)(2,1)} custom-call(bf16[128,1536]{1,0:T(8,128)(2,1)} %fusion.9.block_ref), custom_call_target="tpu_custom_call" | custom-call | tf_op jit(solution)/shard_map/pallas_call | solution.py:76
  168.9 4.7 %convolution_convert_fusion = bf16[512,1152]{1,0:T(8,128)(2,1)S(1)} fusion(bf16[512,1536]{1,0:T(8,128)(2,1)} %bitcast.27, bf16[1536,1152]{0,1:T(8,128)(2,1)} %bitcast.21), kind=kOutput, calls=%fused_computation | convolution fusion | flops 1812529152 | bytes 6291456 | tf_op jit(solution)/shard_map/dot_general | solution.py:288
  173.7 0.9 slice.43.kv_ref
  174.6 0.7 slice.42
  175.3 40.5 %shard_map.68 = bf16[256,384]{1,0:T(8,128)(2,1)} custom-call(s32[1]{0:T(128)} %get-tuple-element.8.length_ref, bf16[256,384]{1,0:T(8,128)(2,1)} %bitcast.32, bf16[512,768]{1,0:T(8,128)(2,1)} %slice.43.kv_ref), custom_call_target="tpu_custom_call" | custom-call | tf_op jit(solution)/shard_map/pallas_call | solution.py:203
  215.8 2.4 convolution_convert_fusion.2.partial_ref
  218.2 31.4 %shard_map.69 = bf16[64,1536]{1,0:T(8,128)(2,1)} custom-call(bf16[256,1536]{1,0:T(8,128)(2,1)} %convolution_convert_fusion.2.partial_ref, bf16[64,1536]{1,0:T(8,128)(2,1)} %shard_map.66.state_ref, f32[1,1536]{1,0:T(1,128)} %convert_element_type.37.gate_ref), custom_call_target="tpu_custom_call" | custom-call | tf_op jit(solution)/shard_map/pallas_call | solution.py:255
  249.6 1.6 copy.9
  (10 shorter events, 0.2 us)
Async XLA Ops:
  0.0 90.5 %copy-start = (bf16[1,384,1536]{2,1,0:T(8,128)(2,1)S(1)}, bf16[1,384,1536]{2,1,0:T(8,128)(2,1)}, u32[]{:S(2)}) copy-start(bf16[1,384,1536]{2,1,0:T(8,128)(2,1)} %param.11) | copy-start | bytes 3538948
  0.0 24.7 %collective-permute-start = (bf16[64,1536]{1,0:T(8,128)(2,1)}, bf16[64,1536]{1,0:T(8,128)(2,1)S(1)}, u32[]{:S(2)}, u32[]{:S(2)}) collective-permute-start(bf16[64,1536]{1,0:T(8,128)(2,1)} %bitcast.22), channel_id=1, source_target_pairs={{0,32},{4,36},{8,40},{12,44},{16,48},{20,52},{24,56},{28,60},{32,0... | collective-permute-start | bytes 589832 | tf_op jit(solution)/shard_map/ppermute | solution.py:284
  17.9 6.1 %copy-start.2 = (s32[8]{0:T(128)S(1)}, s32[8]{0:T(128)}, u32[]{:S(2)}) copy-start(s32[8]{0:T(128)} %param.7) | copy-start | bytes 100
  17.9 6.8 %copy-start.1 = (bf16[1,64,1536]{2,1,0:T(8,128)(2,1)S(1)}, bf16[1,64,1536]{2,1,0:T(8,128)(2,1)}, u32[]{:S(2)}) copy-start(bf16[1,64,1536]{2,1,0:T(8,128)(2,1)} %param.6) | copy-start | bytes 589828
  121.6 25.3 %collective-permute-start.1 = (bf16[64,1536]{1,0:T(8,128)(2,1)}, bf16[64,1536]{1,0:T(8,128)(2,1)S(1)}, u32[]{:S(2)}, u32[]{:S(2)}) collective-permute-start(bf16[64,1536]{1,0:T(8,128)(2,1)} %shard_map.66.state_ref), channel_id=1, source_target_pairs={{0,32},{4,36},{8,40},{12,44},{16,48},{20,52},{24,56},{28,60},{32,0... | collective-permute-start | bytes 589832 | tf_op jit(solution)/shard_map/ppermute | solution.py:284

commit v4 on v3

v4 whole, which is shorter than its diff:
```python
import math

import jax
import jax.numpy as jnp
from jax import lax
from jax.experimental import pallas as pl
from jax.experimental.pallas import tpu as pltpu
from jax.sharding import PartitionSpec as P

HEAD = 128
TICKS = 2
PLANE = 8
MESH = pl.DeviceIdType.MESH
EXP2_SCALE = HEAD ** (-0.5) * math.log2(math.e)


def layer_norm(values):
    row_mean = jnp.mean(values, axis=-1, keepdims=True)
    centered = values - row_mean
    row_var = jnp.mean(centered * centered, axis=-1, keepdims=True)
    return centered / jnp.sqrt(row_var + 1e-06)


def barrier(peers):
    sem = pltpu.get_barrier_semaphore()
    for peer in peers:
        pl.semaphore_signal(sem, inc=1, device_id=peer, device_id_type=MESH)
    pl.semaphore_wait(sem, len(peers))


def remote(src, dst, send_sem, recv_sem, index, peer):
    return pltpu.make_async_remote_copy(
        src_ref=src,
        dst_ref=dst,
        send_sem=send_sem.at[index],
        recv_sem=recv_sem.at[index],
        device_id=peer,
        device_id_type=MESH,
    )


def ring_copies(source, target, here, behind, left, right, rows, send_sem, recv_sem, index):
    first, second = pl.ds(0, rows // 2), pl.ds(rows // 2, rows // 2)
    return {
        "right_first": remote(source.at[first], here(1).at[first], send_sem, recv_sem, index, right),
        "left_second": remote(source.at[second], here(3).at[second], send_sem, recv_sem, index + 1, left),
        "right_second": remote(source.at[second], here(1).at[second], send_sem, recv_sem, index + 2, right),
        "left_first": remote(source.at[first], here(3).at[first], send_sem, recv_sem, index + 3, left),
        "on_right": remote(behind(1).at[first], target(1).at[first], send_sem, recv_sem, index + 4, right),
        "on_left": remote(behind(3).at[second], target(3).at[second], send_sem, recv_sem, index + 5, left),
    }


FIRST_HOPS = ("right_first", "left_second", "right_second", "left_first")


def attend_kernel(
    length_ref, normed_ref, w_ref, o_ref, rows_ref, q_ref, kv_ref, buf, max_ref, sum_ref, acc_ref,
    send_sem, recv_sem, local_sem,
):
    seq = lax.axis_index("seq")
    me = lax.axis_index("head")
    half = lax.div(seq, PLANE)
    y = lax.rem(lax.div(seq, 2), 4)
    core = lax.rem(seq, 2)
    base = half * PLANE
    y_right = {"seq": base + lax.rem(y + 1, 4) * 2 + core}
    y_left = {"seq": base + lax.rem(y + 3, 4) * 2 + core}
    partner = {"seq": base + y * 2 + (1 - core)}
    far = {"seq": lax.rem(seq + PLANE, 2 * PLANE)}
    x_right_at, x_left_at = lax.rem(me + 1, 4), lax.rem(me + 3, 4)
    x_right, x_left = {"head": x_right_at}, {"head": x_left_at}
    tile = normed_ref.shape[0]
    rows = kv_ref.shape[1]
    width = q_ref.shape[1]
    heads = width // HEAD
    length = length_ref[0]

    barrier([x_left, x_right, y_left, y_right, partner, far])

    def x_copies(slot, source, index):
        def own(d):
            return rows_ref.at[slot, me]

        def neighbour(d):
            return rows_ref.at[slot, x_left_at] if d == 1 else rows_ref.at[slot, x_right_at]

        return ring_copies(source, neighbour, own, neighbour, x_left, x_right, tile, send_sem, recv_sem, index)

    def y_copies(slot, index):
        def landing(d):
            return buf.at[d, 0, slot]

        def opposite(d):
            return buf.at[2, 0, slot]

        copies = ring_copies(
            kv_ref.at[slot], opposite, landing, landing, y_left, y_right, rows, send_sem, recv_sem, index
        )
        first, second = pl.ds(0, rows // 2), pl.ds(rows // 2, rows // 2)
        across = {
            "across_own": (kv_ref.at[slot], buf.at[0, 1, slot]),
            "across_left": (buf.at[1, 0, slot], buf.at[1, 1, slot]),
            "across_right": (buf.at[3, 0, slot], buf.at[3, 1, slot]),
            "across_first": (buf.at[2, 0, slot, first], buf.at[2, 1, slot, first]),
            "across_second": (buf.at[2, 0, slot, second], buf.at[2, 1, slot, second]),
        }
        for offset, (name, (source, target)) in enumerate(across.items()):
            copies[name] = remote(source, target, send_sem, recv_sem, index + 6 + offset, partner)
        return copies

    swap = remote(normed_ref, rows_ref.at[1, me], send_sem, recv_sem, 0, far)
    keep = pltpu.make_async_copy(normed_ref, rows_ref.at[0, me], local_sem)
    x_own = x_copies(0, normed_ref, 1)
    x_far = x_copies(1, rows_ref.at[1, me], 7)
    y_own = y_copies(0, 13)
    y_far = y_copies(1, 24)

    def send_first(copies):
        for name in FIRST_HOPS:
            copies[name].start()

    def pass_on(copies):
        copies["right_first"].wait_recv()
        copies["on_right"].start()
        copies["left_second"].wait_recv()
        copies["on_left"].start()

    def rest_of_x(copies):
        for name in ("right_second", "left_first", "on_right", "on_left"):
            copies[name].wait_recv()

    def neighbours_across(copies):
        copies["right_second"].wait_recv()
        copies["across_left"].start()
        copies["left_first"].wait_recv()
        copies["across_right"].start()

    def opposite_across(copies):
        copies["on_right"].wait_recv()
        copies["across_first"].start()
        copies["on_left"].wait_recv()
        copies["across_second"].start()

    def project(slot, group):
        block = rows_ref[slot].reshape(rows, rows_ref.shape[3])
        return jnp.dot(block, w_ref[group], preferred_element_type=jnp.float32).astype(jnp.bfloat16)

    def project_kv(slot):
        def one(part, carry):
            kv_ref[slot, :, pl.ds(pl.multiple_of(part * width, HEAD), width)] = project(slot, part + 1)
            return carry

        lax.fori_loop(0, 2, one, 0)

    def attend_shard(shard, behind, other_core, slot):
        source = lax.rem(y + 4 - behind, 4) * 2 + lax.rem(core + other_core, 2)
        which = half if slot == 0 else 1 - half
        position = lax.broadcasted_iota(jnp.int32, (1, rows), 1) + (which * PLANE + source) * rows
        valid = position < length

        def one_head(h, carry):
            k_columns = pl.ds(pl.multiple_of(h * HEAD, HEAD), HEAD)
            v_columns = pl.ds(pl.multiple_of((heads + h) * HEAD, HEAD), HEAD)
            scores = lax.dot_general(
                q_ref[:, k_columns],
                shard[:, k_columns],
                (((1,), (1,)), ((), ())),
                preferred_element_type=jnp.float32,
            )
            scores = jnp.where(valid, scores * EXP2_SCALE, -1e30)
            old_max = max_ref[h]
            new_max = jnp.maximum(old_max, jnp.max(scores, axis=1, keepdims=True))
            rescale = jnp.exp2(old_max - new_max)
            weights = jnp.exp2(scores - new_max[:, :1])
            max_ref[h] = new_max
            sum_ref[h] = sum_ref[h] * rescale + jnp.sum(weights, axis=1, keepdims=True)
            acc_ref[h] = acc_ref[h] * rescale + jnp.dot(
                weights.astype(jnp.bfloat16), shard[:, v_columns], preferred_element_type=jnp.float32
            )
            return carry

        lax.fori_loop(0, heads, one_head, 0)

    def attend_buf(behind, other_core, slot):
        attend_shard(buf.at[behind, other_core, slot], behind, other_core, slot)

    swap.start()
    send_first(x_own)
    keep.start()
    max_ref[...] = jnp.full_like(max_ref, -1e30)
    sum_ref[...] = jnp.zeros_like(sum_ref)
    acc_ref[...] = jnp.zeros_like(acc_ref)
    pass_on(x_own)
    rest_of_x(x_own)
    keep.wait()
    project_kv(0)
    send_first(y_own)
    y_own["across_own"].start()
    q_ref[...] = project(0, 0)
    attend_shard(kv_ref.at[0], 0, 0, 0)
    pass_on(y_own)
    swap.wait_recv()
    send_first(x_far)
    neighbours_across(y_own)
    y_own["across_own"].wait_recv()
    attend_buf(0, 1, 0)
    pass_on(x_far)
    attend_buf(1, 0, 0)
    attend_buf(3, 0, 0)
    opposite_across(y_own)
    rest_of_x(x_far)
    project_kv(1)
    send_first(y_far)
    y_far["across_own"].start()
    attend_shard(kv_ref.at[1], 0, 0, 1)
    y_own["across_left"].wait_recv()
    attend_buf(1, 1, 0)
    pass_on(y_far)
    y_own["across_right"].wait_recv()
    attend_buf(3, 1, 0)
    attend_buf(2, 0, 0)
    neighbours_across(y_far)
    y_own["across_first"].wait_recv()
    y_own["across_second"].wait_recv()
    attend_buf(2, 1, 0)
    y_far["across_own"].wait_recv()
    attend_buf(0, 1, 1)
    attend_buf(1, 0, 1)
    opposite_across(y_far)
    attend_buf(3, 0, 1)
    y_far["across_left"].wait_recv()
    attend_buf(1, 1, 1)
    y_far["across_right"].wait_recv()
    attend_buf(3, 1, 1)
    attend_buf(2, 0, 1)
    y_far["across_first"].wait_recv()
    y_far["across_second"].wait_recv()
    attend_buf(2, 1, 1)
    for h in range(heads):
        o_ref[:, h * HEAD : (h + 1) * HEAD] = (acc_ref[h] / sum_ref[h]).astype(o_ref.dtype)
    swap.wait_send()
    for copies in (x_own, x_far, y_own, y_far):
        for copy in copies.values():
            copy.wait_send()


def attend(length, normed, weights):
    tile, model_width = normed.shape
    width = weights.shape[2]
    rows = 4 * tile
    vmem = pl.BlockSpec(memory_space=pltpu.VMEM)
    stats = pltpu.VMEM((width // HEAD, rows, HEAD), jnp.float32)
    return pl.pallas_call(
        attend_kernel,
        in_specs=[pl.BlockSpec(memory_space=pltpu.SMEM), vmem, vmem],
        out_specs=vmem,
        out_shape=jax.ShapeDtypeStruct((rows, width), jnp.bfloat16),
        scratch_shapes=[
            pltpu.VMEM((2, 4, tile, model_width), normed.dtype),
            pltpu.VMEM((rows, width), normed.dtype),
            pltpu.VMEM((2, rows, 2 * width), normed.dtype),
            pltpu.VMEM((4, 2, 2, rows, 2 * width), normed.dtype),
            stats,
            stats,
            stats,
            pltpu.SemaphoreType.DMA((35,)),
            pltpu.SemaphoreType.DMA((35,)),
            pltpu.SemaphoreType.DMA,
        ],
        compiler_params=pltpu.CompilerParams(collective_id=1, has_side_effects=True),
    )(length, normed, weights)


def finish_kernel(partial_ref, state_ref, gate_ref, out_ref, landed, updated, send_sem, recv_sem):
    me = lax.axis_index("head")
    position = lax.axis_index("segment")
    rows = state_ref.shape[0]
    ahead = [lax.rem(me + distance, 4) for distance in (1, 2, 3)]
    following = {"segment": lax.rem(position + 1, 8)}
    preceding = {"segment": lax.rem(position + 7, 8)}
    barrier([{"head": peer} for peer in ahead] + [preceding])
    copies = []
    for index in (1, 0, 2):
        piece = pl.ds(pl.multiple_of(ahead[index] * rows, rows), rows)
        copies.append(
            remote(partial_ref.at[piece], landed.at[index], send_sem, recv_sem, index, {"head": ahead[index]})
        )
        copies[-1].start()
    for copy in copies:
        copy.wait_recv()
    mine = pl.ds(pl.multiple_of(me * rows, rows), rows)
    branch = partial_ref[mine, :].astype(jnp.float32)
    for index in range(3):
        branch = branch + landed[index].astype(jnp.float32)
    updated[...] = (state_ref[...].astype(jnp.float32) + gate_ref[...] * branch).astype(updated.dtype)
    onward = remote(updated, out_ref, send_sem, recv_sem, 3, following)
    onward.start()
    for copy in copies:
        copy.wait_send()
    onward.wait()


def finish(partial, state, gate_row):
    vmem = pl.BlockSpec(memory_space=pltpu.VMEM)
    return pl.pallas_call(
        finish_kernel,
        in_specs=[vmem, vmem, vmem],
        out_specs=vmem,
        out_shape=jax.ShapeDtypeStruct(state.shape, state.dtype),
        scratch_shapes=[
            pltpu.VMEM((3,) + state.shape, partial.dtype),
            pltpu.VMEM(state.shape, state.dtype),
            pltpu.SemaphoreType.DMA((4,)),
            pltpu.SemaphoreType.DMA((4,)),
        ],
        compiler_params=pltpu.CompilerParams(collective_id=2, has_side_effects=True),
    )(partial, state, gate_row)


def per_device(tokens, lengths, modulation, gate_gain, w_qkv, w_out):
    segment_count = lax.axis_size("segment")
    position = lax.axis_index("segment")
    shift_scale = modulation[0].astype(jnp.float32)
    gate_row = gate_gain[0].astype(jnp.float32)
    parts_qkv = jnp.transpose(w_qkv[0], (1, 0, 2))
    out_rows = w_out[0]
    own = tokens[0]
    for tick_index in range(TICKS):
        micro_index = (position - tick_index) % segment_count
        length = lax.dynamic_index_in_dim(lengths, micro_index, 0, keepdims=False)
        values = own.astype(jnp.float32)
        normed = (layer_norm(values) * (1.0 + shift_scale[1]) + shift_scale[0]).astype(jnp.bfloat16)
        attended = attend(length[None], normed, parts_qkv)
        partial = jnp.dot(attended, out_rows, preferred_element_type=jnp.float32).astype(jnp.bfloat16)
        own = finish(partial, own, gate_row[None])
    return own[None]


def solution(mesh):
    return jax.shard_map(
        per_device,
        mesh=mesh,
        in_specs=(
            P("segment", ("seq", "head"), None),
            P(),
            P("segment", None, None),
            P("segment", None),
            P("segment", None, None, "head"),
            P("segment", "head", None),
        ),
        out_specs=P("segment", ("seq", "head"), None),
        check_vma=False,
    )
```

time: 252 us -> 192 us (0.76)
  starting transfers between devices: 29.1 us -> 0 us
  waiting for transfers between devices: 12 us -> 0 us
  matrix products: 14.2 us -> 4.75 us
  local copies, waits for them, and re-layouts: 11.7 us -> 3.04 us
    pallas_call x2, Pallas kernels: 79.2 us -> 128 us  [attend(): pl.pallas_call(attend_kernel, in_specs=[pl.BlockSpec(memory_space=pltpu.S...]
    pallas_call x2 -> x0, Pallas kernels: 37.2 us -> none  [head_gather(): pl.pallas_call(head_gather_kernel, out_shape=jax.ShapeDtypeStruct((4, row...]
    ppermute x2 -> x0, starting transfers between devices: 29.1 us -> none  [per_device(): lax.ppermute(own, 'seq', [(i, (i + PLANE) % seq_count) for i in range(seq...]
    pallas_call x2, Pallas kernels: 60 us -> 45.7 us  [finish(): pl.pallas_call(finish_kernel, in_specs=[vmem, vmem, vmem], out_specs=vmem...]
    ppermute x2 -> x0, waiting for transfers between devices: 12 us -> none  [per_device(): lax.ppermute(own, 'seq', [(i, (i + PLANE) % seq_count) for i in range(seq...]
    dot_general x2 -> x0, matrix products: 9.41 us -> none  [per_device(): jnp.dot(rows, flat_qkv, preferred_element_type=jnp.float32)]
    unnamed x8 -> x3, local copies, waits for them, and re-layouts: 7.75 us -> 1.62 us
    slice x6 -> x0, local copies, waits for them, and re-layouts: 3.34 us -> none  [the longest x2 1.86 us: per_device(): attended = attend(length[None], queries, projected[:, local_width:])]
  transfers between devices with their start and end apart: 2 -> 0, of which waited for: 1 -> 0; matrix products, arithmetic and copies ran while one was open for 4% -> 0% of each run, Pallas kernels for 0% -> 0%
where the time goes in v4:
time: 192 us
  Pallas kernels  174 us (91%)
  other arithmetic  9.98 us (5%)
  matrix products  4.75 us (2%)
  local copies, waits for them, and re-layouts  3.04 us (2%)
    pallas_call x2, Pallas kernels, attend(): pl.pallas_call(attend_kernel, in_specs=[pl.BlockSpec(memory_space=pltpu.S...  128 us
    pallas_call x2, Pallas kernels, finish(): pl.pallas_call(finish_kernel, in_specs=[vmem, vmem, vmem], out_specs=vmem...  45.7 us
    dot_general x2, matrix products, per_device(): jnp.dot(attended, out_rows, preferred_element_type=jnp.float32)  4.75 us

profile of v4, /device:TPU:8, one launch (start us, length us, event | category | flops | bytes accessed | tf_op | source)
XLA Modules:
  0.0 191.7 jit_solution(2856450887540368793)
XLA Ops:
  0.0 0.0 copy-start
  0.0 1.4 fusion.15
  1.4 1.1 convert_reduce_fusion.1
  2.5 1.2 fusion.10
  3.7 1.3 convert_element_type.30.gate_ref
  5.0 0.7 convert_element_type.27
  5.7 1.8 fusion.13.normed_ref
  7.4 70.6 %shard_map.64 = bf16[256,384]{1,0:T(8,128)(2,1)} custom-call(s32[1]{0:T(128)} %get-tuple-element.7.length_ref, bf16[64,1536]{1,0:T(8,128)(2,1)} %fusion.13.normed_ref, bf16[3,1536,384]{2,1,0:T(8,128)(2,1)} %bitcast.15), custom_call_target="tpu_custom_call" | custom-call | tf_op jit(solution)/shard_map/pallas_call | solution.py:254
  78.1 0.0 copy-done
  78.1 2.4 %convolution_convert_fusion.1.partial_ref = bf16[256,1536]{1,0:T(8,128)(2,1)} fusion(bf16[256,384]{1,0:T(8,128)(2,1)} %shard_map.64, bf16[1,384,1536]{2,1,0:T(8,128)(2,1)S(1)} %copy-done), kind=kOutput, calls=%fused_computation.1 | convolution fusion | flops 302383104 | bytes 2162688 | tf_op jit(solution)/shard_map/dot_general | solution.py:335
  80.5 22.7 %shard_map.65.state_ref = bf16[64,1536]{1,0:T(8,128)(2,1)} custom-call(bf16[256,1536]{1,0:T(8,128)(2,1)} %convolution_convert_fusion.1.partial_ref, bf16[64,1536]{1,0:T(8,128)(2,1)} %bitcast.17, f32[1,1536]{1,0:T(1,128)} %convert_element_type.30.gate_ref), custom_call_target="tpu_custom_call" | custom-call | tf_op jit(solution)/shard_map/pallas_call | solution.py:306
  103.2 1.1 convert_reduce_fusion
  104.2 1.2 fusion.6
  105.4 1.8 fusion.9.normed_ref
  107.2 57.5 %shard_map.66 = bf16[256,384]{1,0:T(8,128)(2,1)} custom-call(s32[1]{0:T(128)} %get-tuple-element.8.length_ref, bf16[64,1536]{1,0:T(8,128)(2,1)} %fusion.9.normed_ref, bf16[3,1536,384]{2,1,0:T(8,128)(2,1)} %bitcast.16), custom_call_target="tpu_custom_call" | custom-call | tf_op jit(solution)/shard_map/pallas_call | solution.py:254
  164.7 2.4 %convolution_convert_fusion.partial_ref = bf16[256,1536]{1,0:T(8,128)(2,1)} fusion(bf16[256,384]{1,0:T(8,128)(2,1)} %shard_map.66, bf16[1,384,1536]{2,1,0:T(8,128)(2,1)S(1)} %copy-done), kind=kOutput, calls=%fused_computation | convolution fusion | flops 302383104 | bytes 2162688 | tf_op jit(solution)/shard_map/dot_general | solution.py:335
  167.1 22.9 %shard_map.67 = bf16[64,1536]{1,0:T(8,128)(2,1)} custom-call(bf16[256,1536]{1,0:T(8,128)(2,1)} %convolution_convert_fusion.partial_ref, bf16[64,1536]{1,0:T(8,128)(2,1)} %shard_map.65.state_ref, f32[1,1536]{1,0:T(1,128)} %convert_element_type.30.gate_ref), custom_call_target="tpu_custom_call" | custom-call | tf_op jit(solution)/shard_map/pallas_call | solution.py:306
  190.0 1.6 copy.8
  (5 shorter events, 0.1 us)
Async XLA Ops:
  0.0 78.1 %copy-start = (bf16[1,384,1536]{2,1,0:T(8,128)(2,1)S(1)}, bf16[1,384,1536]{2,1,0:T(8,128)(2,1)}, u32[]{:S(2)}) copy-start(bf16[1,384,1536]{2,1,0:T(8,128)(2,1)} %param.11) | copy-start | bytes 3538948

commit v5 on v4

--- a/solution.py
+++ b/solution.py
@@ -19,13 +19,6 @@
     centered = values - row_mean
     row_var = jnp.mean(centered * centered, axis=-1, keepdims=True)
     return centered / jnp.sqrt(row_var + 1e-06)
-
-
-def barrier(peers):
-    sem = pltpu.get_barrier_semaphore()
-    for peer in peers:
-        pl.semaphore_signal(sem, inc=1, device_id=peer, device_id_type=MESH)
-    pl.semaphore_wait(sem, len(peers))
 
 
 def remote(src, dst, send_sem, recv_sem, index, peer):
@@ -54,9 +47,10 @@
 FIRST_HOPS = ("right_first", "left_second", "right_second", "left_first")
 
 
-def attend_kernel(
-    length_ref, normed_ref, w_ref, o_ref, rows_ref, q_ref, kv_ref, buf, max_ref, sum_ref, acc_ref,
-    send_sem, recv_sem, local_sem,
+def layer_kernel(
+    length_ref, state_ref, modulation_ref, gate_ref, w_ref, out_w_ref, o_ref,
+    rows_ref, q_ref, kv_ref, buf, max_ref, sum_ref, acc_ref, attended_ref, part_ref, relay_ref,
+    landed_ref, updated_ref, send_sem, recv_sem,
 ):
     seq = lax.axis_index("seq")
     me = lax.axis_index("head")
@@ -70,13 +64,28 @@
     far = {"seq": lax.rem(seq + PLANE, 2 * PLANE)}
     x_right_at, x_left_at = lax.rem(me + 1, 4), lax.rem(me + 3, 4)
     x_right, x_left = {"head": x_right_at}, {"head": x_left_at}
-    tile = normed_ref.shape[0]
+    x_opposite_at = lax.rem(me + 2, 4)
+    position_at = lax.axis_index("segment")
+    following = {"segment": lax.rem(position_at + 1, 8)}
+    preceding = {"segment": lax.rem(position_at + 7, 8)}
+    tile = state_ref.shape[0]
     rows = kv_ref.shape[1]
     width = q_ref.shape[1]
     heads = width // HEAD
     length = length_ref[0]
 
-    barrier([x_left, x_right, y_left, y_right, partner, far])
+    peers = [x_left, x_right, y_left, y_right, partner, far, preceding]
+    entry = pltpu.get_barrier_semaphore()
+    for peer in peers:
+        pl.semaphore_signal(entry, inc=1, device_id=peer, device_id_type=MESH)
+    values = state_ref[...].astype(jnp.float32)
+    shift = modulation_ref[0:1, :].astype(jnp.float32)
+    scale = modulation_ref[1:2, :].astype(jnp.float32)
+    rows_ref[0, me] = (layer_norm(values) * (1.0 + scale) + shift).astype(rows_ref.dtype)
+    max_ref[...] = jnp.full_like(max_ref, -1e30)
+    sum_ref[...] = jnp.zeros_like(sum_ref)
+    acc_ref[...] = jnp.zeros_like(acc_ref)
+    pl.semaphore_wait(entry, len(peers))
 
     def x_copies(slot, source, index):
         def own(d):
@@ -109,9 +118,10 @@
             copies[name] = remote(source, target, send_sem, recv_sem, index + 6 + offset, partner)
         return copies
 
-    swap = remote(normed_ref, rows_ref.at[1, me], send_sem, recv_sem, 0, far)
-    keep = pltpu.make_async_copy(normed_ref, rows_ref.at[0, me], local_sem)
-    x_own = x_copies(0, normed_ref, 1)
+    top, bottom = pl.ds(0, tile // 2), pl.ds(tile // 2, tile // 2)
+    swap_top = remote(rows_ref.at[0, me, top], rows_ref.at[1, me, top], send_sem, recv_sem, 0, far)
+    swap_bottom = remote(rows_ref.at[0, me, bottom], rows_ref.at[1, me, bottom], send_sem, recv_sem, 35, far)
+    x_own = x_copies(0, rows_ref.at[0, me], 1)
     x_far = x_copies(1, rows_ref.at[1, me], 7)
     y_own = y_copies(0, 13)
     y_far = y_copies(1, 24)
@@ -185,24 +195,24 @@
     def attend_buf(behind, other_core, slot):
         attend_shard(buf.at[behind, other_core, slot], behind, other_core, slot)
 
-    swap.start()
+    swap_top.start()
+    swap_bottom.start()
     send_first(x_own)
-    keep.start()
-    max_ref[...] = jnp.full_like(max_ref, -1e30)
-    sum_ref[...] = jnp.zeros_like(sum_ref)
-    acc_ref[...] = jnp.zeros_like(acc_ref)
     pass_on(x_own)
     rest_of_x(x_own)
-    keep.wait()
     project_kv(0)
     send_first(y_own)
     y_own["across_own"].start()
     q_ref[...] = project(0, 0)
     attend_shard(kv_ref.at[0], 0, 0, 0)
     pass_on(y_own)
-    swap.wait_recv()
-    send_first(x_far)
+    swap_top.wait_recv()
+    x_far["right_first"].start()
+    x_far["left_first"].start()
     neighbours_across(y_own)
+    swap_bottom.wait_recv()
+    x_far["left_second"].start()
+    x_far["right_second"].start()
     y_own["across_own"].wait_recv()
     attend_buf(0, 1, 0)
     pass_on(x_far)
@@ -238,103 +248,94 @@
     y_far["across_second"].wait_recv()
     attend_buf(2, 1, 1)
     for h in range(heads):
-        o_ref[:, h * HEAD : (h + 1) * HEAD] = (acc_ref[h] / sum_ref[h]).astype(o_ref.dtype)
-    swap.wait_send()
+        attended_ref[:, h * HEAD : (h + 1) * HEAD] = (acc_ref[h] / sum_ref[h]).astype(attended_ref.dtype)
+
+    def branch_of(device):
+        block = attended_ref[pl.ds(pl.multiple_of(device * tile, tile), tile), :]
+        return jnp.dot(block, out_w_ref[...], preferred_element_type=jnp.float32)
+
+    to_right = remote(part_ref.at[0, top], relay_ref.at[0], send_sem, recv_sem, 36, x_right)
+    to_left = remote(part_ref.at[0, bottom], relay_ref.at[1], send_sem, recv_sem, 37, x_left)
+    plain_right = remote(part_ref.at[1, bottom], landed_ref.at[0, bottom], send_sem, recv_sem, 38, x_right)
+    plain_left = remote(part_ref.at[2, top], landed_ref.at[1, top], send_sem, recv_sem, 39, x_left)
+    sum_right = remote(part_ref.at[1, top], landed_ref.at[0, top], send_sem, recv_sem, 40, x_right)
+    sum_left = remote(part_ref.at[2, bottom], landed_ref.at[1, bottom], send_sem, recv_sem, 41, x_left)
+    onward = remote(updated_ref, o_ref, send_sem, recv_sem, 42, following)
+    part_ref[0] = branch_of(x_opposite_at).astype(part_ref.dtype)
+    to_right.start()
+    to_left.start()
+    part_ref[1] = branch_of(x_right_at).astype(part_ref.dtype)
+    plain_right.start()
+    part_ref[2] = branch_of(x_left_at).astype(part_ref.dtype)
+    plain_left.start()
+    to_right.wait_recv()
+    part_ref[1, top, :] = (
+        part_ref[1, top, :].astype(jnp.float32) + relay_ref[0].astype(jnp.float32)
+    ).astype(part_ref.dtype)
+    sum_right.start()
+    to_left.wait_recv()
+    part_ref[2, bottom, :] = (
+        part_ref[2, bottom, :].astype(jnp.float32) + relay_ref[1].astype(jnp.float32)
+    ).astype(part_ref.dtype)
+    sum_left.start()
+    branch = branch_of(me)
+    for copy in (plain_right, plain_left, sum_right, sum_left):
+        copy.wait_recv()
+    branch = branch + landed_ref[0].astype(jnp.float32) + landed_ref[1].astype(jnp.float32)
+    updated_ref[...] = (
+        state_ref[...].astype(jnp.float32) + gate_ref[...].astype(jnp.float32) * branch
+    ).astype(updated_ref.dtype)
+    onward.start()
+    for copy in (swap_top, swap_bottom, to_right, to_left, plain_right, plain_left, sum_right, sum_left):
+        copy.wait_send()
     for copies in (x_own, x_far, y_own, y_far):
         for copy in copies.values():
             copy.wait_send()
-
-
-def attend(length, normed, weights):
-    tile, model_width = normed.shape
+    onward.wait()
+
+
+def layer(length, state, modulation, gate, weights, out_weights):
+    tile, model_width = state.shape
     width = weights.shape[2]
     rows = 4 * tile
+    kind = state.dtype
     vmem = pl.BlockSpec(memory_space=pltpu.VMEM)
     stats = pltpu.VMEM((width // HEAD, rows, HEAD), jnp.float32)
     return pl.pallas_call(
-        attend_kernel,
-        in_specs=[pl.BlockSpec(memory_space=pltpu.SMEM), vmem, vmem],
+        layer_kernel,
+        in_specs=[pl.BlockSpec(memory_space=pltpu.SMEM), vmem, vmem, vmem, vmem, vmem],
         out_specs=vmem,
-        out_shape=jax.ShapeDtypeStruct((rows, width), jnp.bfloat16),
+        out_shape=jax.ShapeDtypeStruct(state.shape, kind),
         scratch_shapes=[
-            pltpu.VMEM((2, 4, tile, model_width), normed.dtype),
-            pltpu.VMEM((rows, width), normed.dtype),
-            pltpu.VMEM((2, rows, 2 * width), normed.dtype),
-            pltpu.VMEM((4, 2, 2, rows, 2 * width), normed.dtype),
+            pltpu.VMEM((2, 4, tile, model_width), kind),
+            pltpu.VMEM((rows, width), kind),
+            pltpu.VMEM((2, rows, 2 * width), kind),
+            pltpu.VMEM((4, 2, 2, rows, 2 * width), kind),
             stats,
             stats,
             stats,
-            pltpu.SemaphoreType.DMA((35,)),
-            pltpu.SemaphoreType.DMA((35,)),
-            pltpu.SemaphoreType.DMA,
+            pltpu.VMEM((rows, width), kind),
+            pltpu.VMEM((3, tile, model_width), kind),
+            pltpu.VMEM((2, tile // 2, model_width), kind),
+            pltpu.VMEM((2, tile, model_width), kind),
+            pltpu.VMEM((tile, model_width), kind),
+            pltpu.SemaphoreType.DMA((43,)),
+            pltpu.SemaphoreType.DMA((43,)),
         ],
-        compiler_params=pltpu.CompilerParams(collective_id=1, has_side_effects=True),
-    )(length, normed, weights)
-
-
-def finish_kernel(partial_ref, state_ref, gate_ref, out_ref, landed, updated, send_sem, recv_sem):
-    me = lax.axis_index("head")
-    position = lax.axis_index("segment")
-    rows = state_ref.shape[0]
-    ahead = [lax.rem(me + distance, 4) for distance in (1, 2, 3)]
-    following = {"segment": lax.rem(position + 1, 8)}
-    preceding = {"segment": lax.rem(position + 7, 8)}
-    barrier([{"head": peer} for peer in ahead] + [preceding])
-    copies = []
-    for index in (1, 0, 2):
-        piece = pl.ds(pl.multiple_of(ahead[index] * rows, rows), rows)
-        copies.append(
-            remote(partial_ref.at[piece], landed.at[index], send_sem, recv_sem, index, {"head": ahead[index]})
-        )
-        copies[-1].start()
-    for copy in copies:
-        copy.wait_recv()
-    mine = pl.ds(pl.multiple_of(me * rows, rows), rows)
-    branch = partial_ref[mine, :].astype(jnp.float32)
-    for index in range(3):
-        branch = branch + landed[index].astype(jnp.float32)
-    updated[...] = (state_ref[...].astype(jnp.float32) + gate_ref[...] * branch).astype(updated.dtype)
-    onward = remote(updated, out_ref, send_sem, recv_sem, 3, following)
-    onward.start()
-    for copy in copies:
-        copy.wait_send()
-    onward.wait()
-
-
-def finish(partial, state, gate_row):
-    vmem = pl.BlockSpec(memory_space=pltpu.VMEM)
-    return pl.pallas_call(
-        finish_kernel,
-        in_specs=[vmem, vmem, vmem],
-        out_specs=vmem,
-        out_shape=jax.ShapeDtypeStruct(state.shape, state.dtype),
-        scratch_shapes=[
-            pltpu.VMEM((3,) + state.shape, partial.dtype),
-            pltpu.VMEM(state.shape, state.dtype),
-            pltpu.SemaphoreType.DMA((4,)),
-            pltpu.SemaphoreType.DMA((4,)),
-        ],
-        compiler_params=pltpu.CompilerParams(collective_id=2, has_side_effects=True),
-    )(partial, state, gate_row)
+        compiler_params=pltpu.CompilerParams(collective_id=0, has_side_effects=True),
+    )(length, state, modulation, gate, weights, out_weights)
 
 
 def per_device(tokens, lengths, modulation, gate_gain, w_qkv, w_out):
     segment_count = lax.axis_size("segment")
     position = lax.axis_index("segment")
-    shift_scale = modulation[0].astype(jnp.float32)
-    gate_row = gate_gain[0].astype(jnp.float32)
     parts_qkv = jnp.transpose(w_qkv[0], (1, 0, 2))
-    out_rows = w_out[0]
-    own = tokens[0]
+    state = tokens[0]
     for tick_index in range(TICKS):
         micro_index = (position - tick_index) % segment_count
-        length = lax.dynamic_index_in_dim(lengths, micro_index, 0, keepdims=False)
-        values = own.astype(jnp.float32)
-        normed = (layer_norm(values) * (1.0 + shift_scale[1]) + shift_scale[0]).astype(jnp.bfloat16)
-        attended = attend(length[None], normed, parts_qkv)
-        partial = jnp.dot(attended, out_rows, preferred_element_type=jnp.float32).astype(jnp.bfloat16)
-        own = finish(partial, own, gate_row[None])
-    return own[None]
+        length = lax.dynamic_slice_in_dim(lengths, micro_index, 1, 0)
+        state = layer(length, state, modulation[0], gate_gain, parts_qkv, w_out[0])
+    return state[None]
 
 
 def solution(mesh):

time: 192 us -> 171 us (0.89)
  the two profiles are of different devices: /device:TPU:8 before, /device:TPU:2 now
where the time goes in v5:
time: 171 us
  Pallas kernels  168 us (98%)
  local copies, waits for them, and re-layouts  2.94 us (2%)
    pallas_call x2, Pallas kernels, layer(): pl.pallas_call(layer_kernel, in_specs=[pl.BlockSpec(memory_space=pltpu.SM...  168 us

profile of v5, /device:TPU:2, one launch (start us, length us, event | category | flops | bytes accessed | tf_op | source)
XLA Modules:
  0.0 170.8 jit_solution(5152185088956066872)
XLA Ops:
  0.0 1.3 fusion
  1.3 89.1 %shard_map.64.state_ref = bf16[64,1536]{1,0:T(8,128)(2,1)} custom-call(s32[1]{0:T(128)} %get-tuple-element.5.length_ref, bf16[64,1536]{1,0:T(8,128)(2,1)} %bitcast.12, bf16[2,1536]{1,0:T(2,128)(2,1)} %bitcast.13, bf16[1,1536]{1,0:T(2,128)(2,1)} %gate_ref.3, bf16[3,1536,384]{2,1,0:T(8,128)(2,1)} %bitcast.7, bf16[384,1536]{1,0:T(8,128)(2,1)} %bitcast.9), custom_call_target="tpu_custom_call" | custom-call | tf_op jit(solution)/shard_map/pallas_call | solution.py:304
  90.5 78.7 %shard_map.65 = bf16[64,1536]{1,0:T(8,128)(2,1)} custom-call(s32[1]{0:T(128)} %get-tuple-element.6.length_ref, bf16[64,1536]{1,0:T(8,128)(2,1)} %shard_map.64.state_ref, bf16[2,1536]{1,0:T(2,128)(2,1)} %bitcast.14, bf16[1,1536]{1,0:T(2,128)(2,1)} %gate_ref.3, bf16[3,1536,384]{2,1,0:T(8,128)(2,1)} %bitcast.8, bf16[384,1536]{1,0:T(8,128)(2,1)} %bitcast.10), custom_call_target="tpu_custom_call" | custom-call | tf_op jit(solution)/shard_map/pallas_call | solution.py:304
  169.2 1.6 copy.8

commit v6 on v5

--- a/solution.py
+++ b/solution.py
@@ -47,8 +47,45 @@
 FIRST_HOPS = ("right_first", "left_second", "right_second", "left_first")
 
 
-def layer_kernel(
-    length_ref, state_ref, modulation_ref, gate_ref, w_ref, out_w_ref, o_ref,
+def relay_kernel(
+    length_ref, tokens_ref, modulation_ref, gate_ref, w_ref, out_w_ref, o_ref,
+    states_ref, rows_all, q_ref, kv_ref, buf_all, max_ref, sum_ref, acc_ref, attended_ref, part_ref,
+    relay_all, landed_all, updated_ref, send_all, recv_all,
+):
+    seq = lax.axis_index("seq")
+    me = lax.axis_index("head")
+    base = lax.div(seq, PLANE) * PLANE
+    y = lax.rem(lax.div(seq, 2), 4)
+    core = lax.rem(seq, 2)
+    entry = pltpu.get_barrier_semaphore()
+    peers = [
+        {"head": lax.rem(me + 3, 4)},
+        {"head": lax.rem(me + 1, 4)},
+        {"seq": base + lax.rem(y + 3, 4) * 2 + core},
+        {"seq": base + lax.rem(y + 1, 4) * 2 + core},
+        {"seq": base + y * 2 + (1 - core)},
+        {"seq": lax.rem(seq + PLANE, 2 * PLANE)},
+        {"segment": lax.rem(lax.axis_index("segment") + 7, 8)},
+    ]
+    for peer in peers:
+        pl.semaphore_signal(entry, inc=1, device_id=peer, device_id_type=MESH)
+    states_ref[0] = tokens_ref[...]
+    pl.semaphore_wait(entry, len(peers))
+
+    def tick(t, carry):
+        layer_body(
+            length_ref[lax.rem(lax.axis_index("segment") + 8 - t, 8)], states_ref.at[t], states_ref.at[t + 1], modulation_ref, gate_ref, w_ref, out_w_ref,
+            rows_all.at[t], q_ref, kv_ref, buf_all.at[t], max_ref, sum_ref, acc_ref, attended_ref, part_ref,
+            relay_all.at[t], landed_all.at[t], updated_ref, send_all.at[t], recv_all.at[t],
+        )
+        return carry
+
+    lax.fori_loop(0, TICKS, tick, 0)
+    o_ref[...] = states_ref[TICKS]
+
+
+def layer_body(
+    length, state_ref, next_ref, modulation_ref, gate_ref, w_ref, out_w_ref,
     rows_ref, q_ref, kv_ref, buf, max_ref, sum_ref, acc_ref, attended_ref, part_ref, relay_ref,
     landed_ref, updated_ref, send_sem, recv_sem,
 ):
@@ -67,17 +104,11 @@
     x_opposite_at = lax.rem(me + 2, 4)
     position_at = lax.axis_index("segment")
     following = {"segment": lax.rem(position_at + 1, 8)}
-    preceding = {"segment": lax.rem(position_at + 7, 8)}
     tile = state_ref.shape[0]
     rows = kv_ref.shape[1]
     width = q_ref.shape[1]
     heads = width // HEAD
-    length = length_ref[0]
-
-    peers = [x_left, x_right, y_left, y_right, partner, far, preceding]
-    entry = pltpu.get_barrier_semaphore()
-    for peer in peers:
-        pl.semaphore_signal(entry, inc=1, device_id=peer, device_id_type=MESH)
+
     values = state_ref[...].astype(jnp.float32)
     shift = modulation_ref[0:1, :].astype(jnp.float32)
     scale = modulation_ref[1:2, :].astype(jnp.float32)
@@ -85,7 +116,6 @@
     max_ref[...] = jnp.full_like(max_ref, -1e30)
     sum_ref[...] = jnp.zeros_like(sum_ref)
     acc_ref[...] = jnp.zeros_like(acc_ref)
-    pl.semaphore_wait(entry, len(peers))
 
     def x_copies(slot, source, index):
         def own(d):
@@ -260,7 +290,7 @@
     plain_left = remote(part_ref.at[2, top], landed_ref.at[1, top], send_sem, recv_sem, 39, x_left)
     sum_right = remote(part_ref.at[1, top], landed_ref.at[0, top], send_sem, recv_sem, 40, x_right)
     sum_left = remote(part_ref.at[2, bottom], landed_ref.at[1, bottom], send_sem, recv_sem, 41, x_left)
-    onward = remote(updated_ref, o_ref, send_sem, recv_sem, 42, following)
+    onward = remote(updated_ref, next_ref, send_sem, recv_sem, 42, following)
     part_ref[0] = branch_of(x_opposite_at).astype(part_ref.dtype)
     to_right.start()
     to_left.start()
@@ -294,7 +324,7 @@
     onward.wait()
 
 
-def layer(length, state, modulation, gate, weights, out_weights):
+def relay(length, state, modulation, gate, weights, out_weights):
     tile, model_width = state.shape
     width = weights.shape[2]
     rows = 4 * tile
@@ -302,39 +332,34 @@
     vmem = pl.BlockSpec(memory_space=pltpu.VMEM)
     stats = pltpu.VMEM((width // HEAD, rows, HEAD), jnp.float32)
     return pl.pallas_call(
-        layer_kernel,
+        relay_kernel,
         in_specs=[pl.BlockSpec(memory_space=pltpu.SMEM), vmem, vmem, vmem, vmem, vmem],
         out_specs=vmem,
         out_shape=jax.ShapeDtypeStruct(state.shape, kind),
         scratch_shapes=[
-            pltpu.VMEM((2, 4, tile, model_width), kind),
+            pltpu.VMEM((TICKS + 1, tile, model_width), kind),
+            pltpu.VMEM((TICKS, 2, 4, tile, model_width), kind),
             pltpu.VMEM((rows, width), kind),
             pltpu.VMEM((2, rows, 2 * width), kind),
-            pltpu.VMEM((4, 2, 2, rows, 2 * width), kind),
+            pltpu.VMEM((TICKS, 4, 2, 2, rows, 2 * width), kind),
             stats,
             stats,
             stats,
             pltpu.VMEM((rows, width), kind),
             pltpu.VMEM((3, tile, model_width), kind),
-            pltpu.VMEM((2, tile // 2, model_width), kind),
-            pltpu.VMEM((2, tile, model_width), kind),
+            pltpu.VMEM((TICKS, 2, tile // 2, model_width), kind),
+            pltpu.VMEM((TICKS, 2, tile, model_width), kind),
             pltpu.VMEM((tile, model_width), kind),
-            pltpu.SemaphoreType.DMA((43,)),
-            pltpu.SemaphoreType.DMA((43,)),
+            pltpu.SemaphoreType.DMA((TICKS, 43)),
+            pltpu.SemaphoreType.DMA((TICKS, 43)),
         ],
         compiler_params=pltpu.CompilerParams(collective_id=0, has_side_effects=True),
     )(length, state, modulation, gate, weights, out_weights)
 
 
 def per_device(tokens, lengths, modulation, gate_gain, w_qkv, w_out):
-    segment_count = lax.axis_size("segment")
-    position = lax.axis_index("segment")
     parts_qkv = jnp.transpose(w_qkv[0], (1, 0, 2))
-    state = tokens[0]
-    for tick_index in range(TICKS):
-        micro_index = (position - tick_index) % segment_count
-        length = lax.dynamic_slice_in_dim(lengths, micro_index, 1, 0)
-        state = layer(length, state, modulation[0], gate_gain, parts_qkv, w_out[0])
+    state = relay(lengths, tokens[0], modulation[0], gate_gain, parts_qkv, w_out[0])
     return state[None]
 
 

time: 171 us -> 160 us (0.936)
  the two profiles are of different devices: /device:TPU:2 before, /device:TPU:32 now
where the time goes in v6:
time: 160 us
  Pallas kernels  158 us (99%)
  local copies, waits for them, and re-layouts  1.62 us (1%)
    pallas_call x1, Pallas kernels, relay(): pl.pallas_call(relay_kernel, in_specs=[pl.BlockSpec(memory_space=pltpu.SM...  158 us

profile of v6, /device:TPU:32, one launch (start us, length us, event | category | flops | bytes accessed | tf_op | source)
XLA Modules:
  0.0 159.9 jit_solution(18345851298513579970)
XLA Ops:
  0.0 158.3 %shard_map.64 = bf16[64,1536]{1,0:T(8,128)(2,1)} custom-call(s32[8]{0:T(128)} %length_ref.1, bf16[64,1536]{1,0:T(8,128)(2,1)} %bitcast.10, bf16[2,1536]{1,0:T(2,128)(2,1)} %bitcast.11, bf16[1,1536]{1,0:T(2,128)(2,1)} %gate_ref.1, bf16[3,1536,384]{2,1,0:T(8,128)(2,1)} %bitcast.7, bf16[384,1536]{1,0:T(8,128)(2,1)} %bitcast.8), custom_call_target="tpu_custom_call" | custom-call | tf_op jit(solution)/shard_map/pallas_call | solution.py:334
  158.3 1.6 %copy.8 = bf16[1,64,1536]{2,1,0:T(8,128)(2,1)} copy(bf16[1,64,1536]{2,1,0:T(8,128)(2,1)} %bitcast.9) | data formatting | bytes 393216
